TPU v7x, 512 devices: a whole 4x4x16 slice. The times are simulated.
512 devices in a mesh: row: 32 (over z_lo, y), col: 16 (over z_hi, x, core).
Axes of the slice: x: 4, y: 4, z: 16 (z_hi: 2, z_lo: 8; z = z_hi * 8 + z_lo), core: 2. Of those that a mesh axis runs over, the one named last changes fastest.
Arguments:
- prefill_hidden: bfloat16 [4, 2048, 2880], P(None, 'row', 'col'), may hold values from -6 to 6
- decode_hidden: bfloat16 [128, 2880], P('row', 'col'), may hold values from -6 to 6
- norm_gain: bfloat16 [2880], replicated, may hold values from 0.5 to 1.5
- query_weight: bfloat16 [2880, 4096], P('row', 'col'), may hold values from -0.11388673 to 0.11388673
- kv_weight: bfloat16 [2880, 2, 512], P('row'), may hold values from -0.11388673 to 0.11388673
- out_weight: bfloat16 [4096, 2880], P('col', 'row'), may hold values from -0.09375 to 0.09375
- sink_logits: bfloat16 [64], P('col'), may hold values from -4 to 4
- key_pool: bfloat16 [768, 64, 512], P('row'), may hold values from -6 to 6
- value_pool: bfloat16 [768, 64, 512], P('row'), may hold values from -6 to 6
- lengths: int32 [32, 4], P('row'), may hold values from 1 to 384, 960 in all within a row
- page_table: int32 [32, 24], P('row'), may hold values from 0 to 23, each once within a row
Outputs:
- prefill_out: bfloat16 [4, 2048, 2880], P(None, 'row', 'col')
- decode_out: bfloat16 [128, 2880], P('row', 'col')
Inputs may be any that keep to these rules, and one draw needn't show every extreme that they name: The 4 cached lengths of one index of row sum to 960, and some request has length 384. `page_table`: each line lists every local page of one index of row exactly once; request r % 4 of that index owns entries (r % 4) * 6 to (r % 4 + 1) * 6 - 1.
All inputs are finite; a program needn't handle non-finite values.
Results may differ from a plain program's by a relative error of at most 0.012.
Values may be sent and summed in bfloat16 or wider, within the bound.
A program may use at most 64 MiB of HBM per device.

v0:
```python
import math

import jax
import jax.numpy as jnp
from jax import lax
from jax.sharding import PartitionSpec as P

HQ = 64
KV = 8
HD = 64


def normed(token_rows, norm_gain):
    widened = token_rows.astype(jnp.float32)
    inverse = lax.rsqrt(jnp.mean(widened * widened, axis=-1, keepdims=True) + 1e-05)
    return (widened * inverse * norm_gain.astype(jnp.float32)).astype(jnp.bfloat16)


def body(
    prefill_hidden,
    decode_hidden,
    norm_gain,
    query_weight,
    kv_weight,
    out_weight,
    sink_logits,
    key_pool,
    value_pool,
    lengths,
    page_table,
):
    spans, span_rows, col_width = prefill_hidden.shape
    decode_rows = decode_hidden.shape[0]
    prefill_count = spans * span_rows
    token_rows = jnp.concatenate(
        [prefill_hidden.reshape(prefill_count, col_width), decode_hidden], axis=0
    )
    features = lax.all_gather(token_rows, "col", axis=1, tiled=True)
    hidden = normed(features, norm_gain)
    heads_dev = query_weight.shape[1] // HD
    group_size = HQ // KV
    kv_dev = max(1, heads_dev // group_size)
    per_kv = heads_dev // kv_dev
    col_index = lax.axis_index("col")
    row_index = lax.axis_index("row")
    kv_first = col_index * heads_dev // group_size
    kv_columns = lax.dynamic_slice_in_dim(kv_weight, kv_first * HD, kv_dev * HD, 2).reshape(
        kv_weight.shape[0], 2 * kv_dev * HD
    )
    query_full, kv_full = (
        lax.all_gather(query_weight, "row", axis=0, tiled=True),
        lax.all_gather(kv_columns, "row", axis=0, tiled=True),
    )
    query_sum = jnp.dot(hidden, query_full, preferred_element_type=jnp.float32)
    kv_sum = jnp.dot(hidden, kv_full, preferred_element_type=jnp.float32)
    queries = query_sum.astype(jnp.bfloat16)
    key_rows = kv_sum[:, : kv_dev * HD].astype(jnp.bfloat16)
    value_rows = kv_sum[:, kv_dev * HD :].astype(jnp.bfloat16)
    score_scale = 1.0 / math.sqrt(HD)
    sink_grid = sink_logits.astype(jnp.float32).reshape(kv_dev, per_kv)
    query_pre = queries[:prefill_count].reshape(spans, span_rows, kv_dev, per_kv, HD)
    key_pre = key_rows[:prefill_count].reshape(spans, span_rows, kv_dev * HD)
    value_pre = value_rows[:prefill_count].reshape(spans, span_rows, kv_dev * HD)
    positions = row_index * span_rows + jnp.arange(span_rows, dtype=jnp.int32)
    state_shape = (spans, kv_dev, per_kv, span_rows)
    pieces = (
        lax.all_gather(key_pre, "row", axis=1, tiled=True),
        lax.all_gather(value_pre, "row", axis=1, tiled=True),
    )
    running = jnp.broadcast_to(sink_grid[None, :, :, None], state_shape)
    denominator = jnp.ones(state_shape, jnp.float32)
    weighted = jnp.zeros(state_shape + (HD,), jnp.float32)
    piece_len = pieces[0].shape[1]
    key_piece = pieces[0].reshape(spans, piece_len, kv_dev, HD)
    value_piece = pieces[1].reshape(spans, piece_len, kv_dev, HD)
    scores = (
        jnp.einsum("nqkgd,npkd->nkgqp", query_pre, key_piece, preferred_element_type=jnp.float32)
        * score_scale
    )
    key_pos = jnp.arange(piece_len, dtype=jnp.int32)
    allowed = key_pos[None, :] <= positions[:, None]
    scores = jnp.where(allowed, scores, -jnp.inf)
    newest = jnp.maximum(running, jnp.max(scores, axis=-1))
    probs_soft = jnp.exp(scores - newest[..., None])
    factor = jnp.exp(running - newest)
    denominator = denominator * factor + jnp.sum(probs_soft, axis=-1)
    weighted = weighted * factor[..., None] + jnp.einsum(
        "nkgqp,npkd->nkgqd",
        probs_soft.astype(jnp.bfloat16),
        value_piece,
        preferred_element_type=jnp.float32,
    )
    running, denominator, weighted = (newest, denominator, weighted)
    prefill_att = (
        (weighted / denominator[..., None])
        .transpose(0, 3, 1, 2, 4)
        .reshape(prefill_count, heads_dev * HD)
        .astype(jnp.bfloat16)
    )
    query_dec = queries[prefill_count:].reshape(decode_rows, kv_dev, per_kv, HD)
    key_new = key_rows[prefill_count:].reshape(decode_rows, kv_dev, HD)
    value_new = value_rows[prefill_count:].reshape(decode_rows, kv_dev, HD)
    pool_pages, page_len, pool_width = key_pool.shape
    table = page_table.reshape(decode_rows, -1)
    max_pages = table.shape[1]
    key_mine = lax.dynamic_slice_in_dim(
        key_pool.reshape(pool_pages, page_len, KV, HD), kv_first, kv_dev, 2
    )
    value_mine = lax.dynamic_slice_in_dim(
        value_pool.reshape(pool_pages, page_len, KV, HD), kv_first, kv_dev, 2
    )
    key_cache = key_mine[table].reshape(decode_rows, max_pages * page_len, kv_dev, HD)
    value_cache = value_mine[table].reshape(decode_rows, max_pages * page_len, kv_dev, HD)
    cache_scores = (
        jnp.einsum("skgd,stkd->skgt", query_dec, key_cache, preferred_element_type=jnp.float32)
        * score_scale
    )
    live = (
        jnp.arange(max_pages * page_len, dtype=jnp.int32)[None, :]
        < lengths.reshape(decode_rows)[:, None]
    )
    cache_scores = jnp.where(live[:, None, None, :], cache_scores, -jnp.inf)
    self_scores = (
        jnp.einsum("skgd,skd->skg", query_dec, key_new, preferred_element_type=jnp.float32)
        * score_scale
    )
    highest = jnp.maximum(jnp.maximum(jnp.max(cache_scores, axis=-1), self_scores), sink_grid[None])
    cache_probs = jnp.exp(cache_scores - highest[..., None])
    self_probs = jnp.exp(self_scores - highest)
    denom_dec = jnp.sum(cache_probs, axis=-1) + self_probs + jnp.exp(sink_grid[None] - highest)
    decode_sum = jnp.einsum(
        "skgt,stkd->skgd",
        cache_probs.astype(jnp.bfloat16),
        value_cache,
        preferred_element_type=jnp.float32,
    )
    decode_sum = (
        decode_sum
        + self_probs.astype(jnp.bfloat16).astype(jnp.float32)[..., None]
        * value_new.astype(jnp.float32)[:, :, None, :]
    )
    decode_att = (
        (decode_sum / denom_dec[..., None])
        .reshape(decode_rows, heads_dev * HD)
        .astype(jnp.bfloat16)
    )
    attended = jnp.concatenate([prefill_att, decode_att], axis=0)
    partial_out = jnp.dot(
        attended,
        lax.all_gather(out_weight, "row", axis=1, tiled=True),
        preferred_element_type=jnp.float32,
    )
    summed = lax.psum_scatter(
        partial_out.astype(jnp.bfloat16), "col", scatter_dimension=1, tiled=True
    ).astype(jnp.float32)
    result = (token_rows.astype(jnp.float32) + summed).astype(jnp.bfloat16)
    return (result[:prefill_count].reshape(spans, span_rows, col_width), result[prefill_count:])


def solution(mesh):
    in_specs = (
        P(None, "row", "col"),
        P("row", "col"),
        P(),
        P("row", "col"),
        P("row", None, None),
        P("col", "row"),
        P("col"),
        P("row", None, None),
        P("row", None, None),
        P("row", None),
        P("row", None),
    )
    out_specs = (P(None, "row", "col"), P("row", "col"))
    return jax.shard_map(body, mesh=mesh, in_specs=in_specs, out_specs=out_specs, check_vma=False)
```

profile of v0, /device:TPU:1, one launch (start us, length us, event | category | flops | bytes accessed | tf_op | source)
XLA Modules:
  0.0 1276.0 jit_solution(622490899157801376)
XLA Ops:
  7.2 1.6 fusion.37
  8.9 0.7 all-gather.16.cloned.1.call-update
  9.7 0.7 all-gather.18.cloned.1.call-update
  10.5 0.1 constant_dynamic-slice_fusion.2
  10.7 0.1 copy.43
  10.8 126.2 %all-gather.1 = bf16[32,90,128]{2,1,0:T(8,128)(2,1)S(1)} all-gather(bf16[1,90,128]{2,1,0:T(8,128)(2,1)S(1)} %copy.43), channel_id=1, replica_groups=mesh['row'=32,'col'=16] {'row'}, dimensions={0}, use_global_device_ids=true | all-gather | bytes 760320 | tf_op jit(solution)/shard_map/all_gather | solution.py:52
  137.0 1.1 reshape.266
  138.1 4.2 copy_convert_fusion
  142.3 4.4 reshape.272
  146.7 0.3 multiply_reduce_fusion
  147.0 0.8 copy-done.2
  147.8 0.7 convolution_convert_fusion.2
  148.5 0.7 fusion.51
  149.4 5.1 reshape.231
  154.5 5.2 reshape.234
  159.7 5.5 constant_dynamic-slice_fusion
  165.1 0.8 copy.72
  166.0 0.5 broadcast.133
  166.5 0.7 reduce.10
  167.3 2.0 copy.71
  169.3 2.4 gather_fusion
  171.7 2.4 gather_fusion.1
  174.1 0.1 iota_compare_fusion
  174.3 0.2 all-reduce.3.cloned.1.call-start
  174.6 128.9 %all-gather.16.cloned.1.call-done = bf16[32,90,256]{2,1,0:T(8,128)(2,1)} async-done(((bf16[1,90,256]{2,1,0:T(8,128)(2,1)}), bf16[32,90,256]{2,1,0:T(8,128)(2,1)}) %all-gather.16.cloned.1.call-update) | async-done | bytes 1474576 | tf_op jit(solution)/shard_map/all_gather | solution.py:51
  303.5 3.4 reshape.268
  306.9 2.1 convolution_convert_fusion.1
  309.0 0.2 reshape.227
  309.2 0.1 fusion.44
  309.4 1.3 fusion.52
  310.7 0.2 fusion.38
  310.9 1.2 fusion.17
  312.2 214.0 %all-gather.18.cloned.1.call-done = bf16[32,90,256]{2,1,0:T(8,128)(2,1)} async-done(((bf16[1,90,256]{2,1,0:T(8,128)(2,1)}), bf16[32,90,256]{2,1,0:T(8,128)(2,1)}) %all-gather.18.cloned.1.call-update) | async-done | bytes 1474576 | tf_op jit(solution)/shard_map/all_gather | solution.py:150
  526.2 2.3 reshape.270
  528.6 221.9 %all-gather.10.cloned.1.call-done = bf16[4,2048,64]{2,1,0:T(8,128)(2,1)} async-done(((bf16[4,64,64]{2,1,0:T(8,128)(2,1)}), bf16[4,2048,64]{2,1,0:T(8,128)(2,1)}) %all-gather.10.cloned.1.call-update) | async-done | bytes 1048592 | tf_op jit(solution)/shard_map/all_gather | solution.py:67
  750.5 3.1 fusion.2
  753.7 2.2 fusion
  755.8 1.0 copy-done.1
  756.9 217.0 %all-gather.12.cloned.1.call-done = bf16[4,2048,64]{2,1,0:T(8,128)(2,1)} async-done(((bf16[4,64,64]{2,1,0:T(8,128)(2,1)}), bf16[4,2048,64]{2,1,0:T(8,128)(2,1)}) %all-gather.12.cloned.1.call-update) | async-done | bytes 1048592 | tf_op jit(solution)/shard_map/all_gather | solution.py:68
  973.9 6.2 fusion.28
  980.0 0.2 copy.45
  980.3 0.2 convert_element_type.76
  980.5 1.8 convolution_convert_fusion
  982.3 1.3 dynamic-slice
  984.2 282.6 %all-reduce.3.cloned.1.call-done = bf16[260,2880]{1,0:T(8,128)(2,1)} async-done(((bf16[260,2880]{1,0:T(8,128)(2,1)}), bf16[260,2880]{1,0:T(8,128)(2,1)}) %all-reduce.3.cloned.1.call-update) | async-done | bytes 1497616
  1266.8 1.0 add_convert_fusion
  1267.9 0.7 slice.50
  1268.6 0.6 slice.51
  (45 shorter events, 1.1 us)
Async XLA Ops:
  7.2 3.3 copy-start
  7.2 130.9 %copy-start.5 = (bf16[2880]{0:T(1024)(128)(2,1)S(1)}, bf16[2880]{0:T(1024)(128)(2,1)}, u32[]{:S(2)}) copy-start(bf16[2880]{0:T(1024)(128)(2,1)} %param.13) | copy-start | bytes 17284
  7.2 130.9 %all-gather.14.cloned.1.call-start = ((), (), s32[]{:S(2)}) async-start(), calls=%async_computation.2 | async-start | bytes 2297856 | tf_op jit(solution)/shard_map/all_gather | solution.py:38
  8.9 294.6 %all-gather.16.cloned.1.call-start = ((), (), s32[]{:S(2)}) async-start(), calls=%async_computation.3 | async-start | bytes 1622016 | tf_op jit(solution)/shard_map/all_gather | solution.py:51
  9.6 516.6 %all-gather.18.cloned.1.call-start = ((), (), s32[]{:S(2)}) async-start(), calls=%async_computation.4 | async-start | bytes 1622016 | tf_op jit(solution)/shard_map/all_gather | solution.py:150
  10.4 740.1 %all-gather.10.cloned.1.call-start = ((), (), s32[]{:S(2)}) async-start(), calls=%async_computation | async-start | bytes 2162688 | tf_op jit(solution)/shard_map/all_gather | solution.py:67
  146.7 1.1 copy-start.2
  146.7 2.6 copy-start.7
  149.3 824.6 %all-gather.12.cloned.1.call-start = ((), (), s32[]{:S(2)}) async-start(), calls=%async_computation.1 | async-start | bytes 2162688 | tf_op jit(solution)/shard_map/all_gather | solution.py:68
  159.7 6.8 copy-start.8
  159.7 14.4 %copy-start.6 = (s32[1,4]{1,0:T(1,128)S(1)}, s32[1,4]{1,0:T(1,128)}, u32[]{:S(2)}) copy-start(s32[1,4]{1,0:T(1,128)} %param.20) | copy-start | bytes 52
  174.3 1092.5 %all-reduce.3.cloned.1.call-start = ((), (), s32[]{:S(2)}) async-start(), calls=%async_computation.5 | async-start | bytes 3108864
  753.6 3.2 copy-start.1
  980.5 286.4 %copy-start.3 = (bf16[4,64,180]{2,1,0:T(8,128)(2,1)S(1)}, bf16[4,64,180]{2,1,0:T(8,128)(2,1)}, u32[]{:S(2)}) copy-start(bf16[4,64,180]{2,1,0:T(8,128)(2,1)} %param.11) | copy-start | bytes 276484
  980.5 286.4 %copy-start.4 = (bf16[4,180]{1,0:T(4,128)(2,1)S(1)}, bf16[4,180]{1,0:T(4,128)(2,1)}, u32[]{:S(2)}) copy-start(bf16[4,180]{1,0:T(4,128)(2,1)} %param.12) | copy-start | bytes 4324
Sparse Core Ops, SparseCore 0:
  11.2 99.8 all-gather.13
  113.1 190.3 all-gather.15
  305.6 220.6 all-gather.17
  528.8 221.7 all-gather.9
  752.4 221.4 all-gather.11
  982.4 284.3 all-reduce.2
where the time goes:
time: 1280 us
  waiting for transfers between devices  1070 us (84%)
  blocking collectives  126 us (10%)
  local copies, waits for them, and re-layouts  41.3 us (3%)
  matrix products  16.5 us (1%)
  between operations  15 us (1%)
    unnamed x7, waiting for transfers between devices  284 us
    all_gather x1, waiting for transfers between devices, body(): lax.all_gather(key_pre, 'row', axis=1, tiled=True)  222 us
    all_gather x1, waiting for transfers between devices, body(): lax.all_gather(value_pre, 'row', axis=1, tiled=True)  217 us
    all_gather x1, waiting for transfers between devices, body(): lax.all_gather(out_weight, 'row', axis=1, tiled=True)  214 us
    all_gather x1, waiting for transfers between devices, body(): lax.all_gather(query_weight, 'row', axis=0, tiled=True)  129 us
    all_gather x1, blocking collectives, body(): lax.all_gather(kv_columns, 'row', axis=0, tiled=True)  126 us
  transfers between devices with their start and end apart: 6, of which 5 were waited for; matrix products, arithmetic and copies ran while one was open for 4% of the time, Pallas kernels for 0%

commit v1 on v0

--- a/solution.py
+++ b/solution.py
@@ -3,16 +3,404 @@
 import jax
 import jax.numpy as jnp
 from jax import lax
+from jax.experimental import pallas as pl
+from jax.experimental.pallas import tpu as pltpu
 from jax.sharding import PartitionSpec as P
 
 HQ = 64
 KV = 8
 HD = 64
-
-
-def normed(token_rows, norm_gain):
+ZL = 8
+YN = 4
+XN = 4
+TOK = 272
+HALF = TOK // 2
+FOLD = TOK + HALF
+FEAT = 192
+MESH = pl.DeviceIdType.MESH
+ROW_COPIES = 64
+COL_COPIES = 24
+
+
+def fold(rows):
+    tail = jnp.concatenate([rows[:HALF, 128:FEAT], rows[HALF:, 128:FEAT]], axis=1)
+    return jnp.concatenate([rows[:, :128], tail], axis=0)
+
+
+def unfold(folded):
+    head, tail = folded[..., :TOK, :], folded[..., TOK:, :]
+    tail = jnp.concatenate([tail[..., :64], tail[..., 64:]], axis=-2)
+    return jnp.concatenate([head, tail], axis=-1)
+
+
+class Sender:
+    def __init__(self, send_sem, recv_sem):
+        self.send_sem, self.recv_sem = send_sem, recv_sem
+        self.started = []
+
+    def copy(self, index, src, dst, device):
+        return pltpu.make_async_remote_copy(
+            src_ref=src(),
+            dst_ref=dst(),
+            send_sem=self.send_sem.at[index],
+            recv_sem=self.recv_sem.at[index],
+            device_id=device,
+            device_id_type=MESH,
+        )
+
+    def run(self, cond, action):
+        if cond is None:
+            action()
+        else:
+            pl.when(cond)(action)
+
+    def send(self, index, src, dst, device, cond=None):
+        self.run(cond, lambda: self.copy(index, src, dst, device).start())
+        self.started.append((index, src, dst, device, cond))
+
+    def arrive(self, index, slot, device, cond=None):
+        self.run(cond, lambda: self.copy(index, slot, slot, device).wait_recv())
+
+    def finish(self):
+        for index, src, dst, device, cond in self.started:
+            self.run(cond, lambda: self.copy(index, src, dst, device).wait_send())
+
+
+def greet(pairs):
+    barrier = pltpu.get_barrier_semaphore()
+    for device, cond in pairs:
+        def hello(device=device):
+            pl.semaphore_signal(barrier, inc=1, device_id=device, device_id_type=MESH)
+
+        if cond is None:
+            hello()
+        else:
+            pl.when(cond)(hello)
+    peers = sum(1 if cond is None else cond.astype(jnp.int32) for _, cond in pairs)
+    pl.semaphore_wait(barrier, peers)
+
+
+class RowGather:
+    def __init__(self, block, out, send_sem, recv_sem):
+        row, col = lax.axis_index("row"), lax.axis_index("col")
+        self.row = row
+        self.z, self.y = row // YN, lax.rem(row, YN)
+        self.block, self.out = block, out
+        self.up = (row + YN, col)
+        self.down = (row - YN, col)
+        self.has_up = self.z < ZL - 1
+        self.has_down = self.z > 0
+        self.after = (self.z * YN + lax.rem(self.y + 1, YN), col)
+        self.before = (self.z * YN + lax.rem(self.y + YN - 1, YN), col)
+        self.net = Sender(send_sem, recv_sem)
+
+    def partners(self):
+        return [
+            (self.up, self.has_up),
+            (self.down, self.has_down),
+            (self.after, None),
+            (self.before, None),
+        ]
+
+    def slot(self, z, shift):
+        return lambda: self.out.at[z * YN + lax.rem(self.y + shift + YN, YN)]
+
+    def events(self, distance):
+        events = [(0, self.z - distance, self.z - distance >= 0)]
+        if distance > 0:
+            events.append((1, self.z + distance, self.z + distance < ZL))
+        return events
+
+    def along_z(self, distance):
+        for way, z, exists in self.events(distance):
+            mine = self.slot(z, 0)
+            src = mine
+            if distance == 0:
+                src = lambda: self.block
+            else:
+                self.net.arrive(way * 8 + distance, mine, self.down if way == 0 else self.up, exists)
+            if distance < ZL - 1:
+                if way == 0:
+                    self.net.send(
+                        distance + 1, src, mine, self.up, jnp.logical_and(exists, self.has_up)
+                    )
+                if way == 1 or distance == 0:
+                    self.net.send(
+                        8 + distance + 1, src, mine, self.down, jnp.logical_and(exists, self.has_down)
+                    )
+            cond = None if distance == 0 else exists
+            self.net.send(16 + way * 8 + distance, src, mine, self.after, cond)
+            self.net.send(32 + way * 8 + distance, src, mine, self.before, cond)
+
+    def along_y(self, distance):
+        for way, z, exists in self.events(distance):
+            cond = None if distance == 0 else exists
+            index = way * 8 + distance
+            self.net.arrive(16 + index, self.slot(z, -1), self.before, cond)
+            if distance % 2 == 0:
+                self.net.send(48 + index, self.slot(z, -1), self.slot(z, -1), self.after, cond)
+            self.net.arrive(32 + index, self.slot(z, 1), self.after, cond)
+            if distance % 2 == 1:
+                self.net.send(48 + index, self.slot(z, 1), self.slot(z, 1), self.before, cond)
+
+    def last(self):
+        for distance in range(ZL):
+            for way, z, exists in self.events(distance):
+                cond = None if distance == 0 else exists
+                source = self.before if distance % 2 == 0 else self.after
+                self.net.arrive(48 + way * 8 + distance, self.slot(z, 2), source, cond)
+        self.net.finish()
+
+
+class ColGather:
+    def __init__(self, block, out, send_sem, recv_sem):
+        row, col = lax.axis_index("row"), lax.axis_index("col")
+        self.high, self.x, self.core = col // (2 * XN), lax.rem(col // 2, XN), lax.rem(col, 2)
+        self.block, self.out = block, out
+        self.mate = (row, self.at(1, 0, 0))
+        self.after = (row, self.at(0, 1, 0))
+        self.before = (row, self.at(0, -1, 0))
+        self.sibling = (row, self.at(0, 0, 1))
+        self.net = Sender(send_sem, recv_sem)
+
+    def partners(self):
+        return [(self.mate, None), (self.after, None), (self.before, None), (self.sibling, None)]
+
+    def at(self, high, shift, core):
+        return (
+            lax.rem(self.high + high, 2) * (2 * XN)
+            + lax.rem(self.x + shift + XN, XN) * 2
+            + lax.rem(self.core + core, 2)
+        )
+
+    def slot(self, high, shift, core=0):
+        return lambda: self.out.at[self.at(high, shift, core)]
+
+    def own(self, high):
+        slot = self.slot(high, 0)
+        src = slot
+        if high == 0:
+            src = lambda: self.block
+            self.net.send(0, src, slot, self.mate)
+        else:
+            self.net.arrive(0, slot, self.mate)
+        self.net.send(1 + high, src, slot, self.after)
+        self.net.send(3 + high, src, slot, self.before)
+        self.net.send(8 + high * 4, src, slot, self.sibling)
+
+    def ring(self, high):
+        self.net.arrive(1 + high, self.slot(high, -1), self.before)
+        if high == 0:
+            self.net.send(5, self.slot(high, -1), self.slot(high, -1), self.after)
+        self.net.send(8 + high * 4 + 3, self.slot(high, -1), self.slot(high, -1), self.sibling)
+        self.net.arrive(3 + high, self.slot(high, 1), self.after)
+        if high == 1:
+            self.net.send(6, self.slot(high, 1), self.slot(high, 1), self.before)
+        self.net.send(8 + high * 4 + 1, self.slot(high, 1), self.slot(high, 1), self.sibling)
+
+    def far(self, high):
+        self.net.arrive(5 + high, self.slot(high, 2), self.before if high == 0 else self.after)
+        self.net.send(8 + high * 4 + 2, self.slot(high, 2), self.slot(high, 2), self.sibling)
+
+    def last(self):
+        for high in range(2):
+            for shift in range(XN):
+                self.net.arrive(8 + high * 4 + shift, self.slot(high, shift, 1), self.sibling)
+        self.net.finish()
+
+
+def gather_kernel(
+    weight_ref, token_ref, all_weight, all_token, rs, rr, cs, cr, local_sem
+):
+    rows = RowGather(weight_ref, all_weight, rs, rr)
+    cols = ColGather(token_ref, all_token, cs, cr)
+    greet(rows.partners() + cols.partners())
+    cols.own(0)
+    rows.along_z(0)
+    own_weight = pltpu.make_async_copy(weight_ref, all_weight.at[rows.row], local_sem.at[0])
+    own_token = pltpu.make_async_copy(
+        token_ref, all_token.at[lax.axis_index("col")], local_sem.at[1]
+    )
+    own_weight.start()
+    own_token.start()
+    rows.along_z(1)
+    rows.along_y(0)
+    cols.ring(0)
+    rows.along_z(2)
+    rows.along_y(1)
+    cols.own(1)
+    rows.along_z(3)
+    rows.along_y(2)
+    cols.far(0)
+    rows.along_z(4)
+    rows.along_y(3)
+    cols.ring(1)
+    rows.along_z(5)
+    rows.along_y(4)
+    cols.far(1)
+    rows.along_z(6)
+    rows.along_y(5)
+    rows.along_z(7)
+    rows.along_y(6)
+    rows.along_y(7)
+    cols.last()
+    rows.last()
+    own_weight.wait()
+    own_token.wait()
+
+
+def vmem():
+    return pl.BlockSpec(memory_space=pltpu.VMEM)
+
+
+def gather_first(weight_block, token_block):
+    return pl.pallas_call(
+        gather_kernel,
+        out_shape=(
+            jax.ShapeDtypeStruct((ZL * YN,) + weight_block.shape, jnp.bfloat16),
+            jax.ShapeDtypeStruct((4 * XN,) + token_block.shape, jnp.bfloat16),
+        ),
+        in_specs=[vmem()] * 2,
+        out_specs=(vmem(), vmem()),
+        scratch_shapes=[
+            pltpu.SemaphoreType.DMA((ROW_COPIES,)),
+            pltpu.SemaphoreType.DMA((ROW_COPIES,)),
+            pltpu.SemaphoreType.DMA((COL_COPIES,)),
+            pltpu.SemaphoreType.DMA((COL_COPIES,)),
+            pltpu.SemaphoreType.DMA((2,)),
+        ],
+        compiler_params=pltpu.CompilerParams(
+            collective_id=0, has_side_effects=True, vmem_limit_bytes=40 * 1024 * 1024
+        ),
+    )(weight_block, token_block)
+
+
+def kv_kernel(block_ref, out_ref, send_sem, recv_sem, local_sem):
+    rows = RowGather(block_ref, out_ref, send_sem, recv_sem)
+    greet(rows.partners())
+    rows.along_z(0)
+    own = pltpu.make_async_copy(block_ref, out_ref.at[rows.row], local_sem.at[0])
+    own.start()
+    for distance in range(1, ZL):
+        rows.along_z(distance)
+        rows.along_y(distance - 1)
+    rows.along_y(ZL - 1)
+    rows.last()
+    own.wait()
+
+
+def gather_kv(block):
+    return pl.pallas_call(
+        kv_kernel,
+        out_shape=jax.ShapeDtypeStruct((ZL * YN,) + block.shape, jnp.bfloat16),
+        in_specs=[vmem()],
+        out_specs=vmem(),
+        scratch_shapes=[
+            pltpu.SemaphoreType.DMA((ROW_COPIES,)),
+            pltpu.SemaphoreType.DMA((ROW_COPIES,)),
+            pltpu.SemaphoreType.DMA((1,)),
+        ],
+        compiler_params=pltpu.CompilerParams(
+            collective_id=1, has_side_effects=True, vmem_limit_bytes=40 * 1024 * 1024
+        ),
+    )(block)
+
+
+ORDER = ((1, 2), (0, 2), (1, 1), (1, 3), (0, 3), (0, 1), (1, 0), (0, 0))
+
+
+def out_kernel(
+    att_ref, weight_ref, token_ref, out_ref, first, landed, second, ring, keep, mate_out, mate_in,
+    send_sem, recv_sem,
+):
+    row, col = lax.axis_index("row"), lax.axis_index("col")
+    high, x, core = col // (2 * XN), lax.rem(col // 2, XN), lax.rem(col, 2)
+
+    def at(dh, dx, dc):
+        return (
+            lax.rem(high + dh, 2) * (2 * XN) + lax.rem(x + dx + XN, XN) * 2 + lax.rem(core + dc, 2)
+        )
+
+    mate, after, before, sibling = (
+        (row, at(1, 0, 0)), (row, at(0, 1, 0)), (row, at(0, -1, 0)), (row, at(0, 0, 1)),
+    )
+    greet([(mate, None), (after, None), (before, None), (sibling, None)])
+    net = Sender(send_sem, recv_sem)
+
+    def share(block):
+        columns = pl.ds(384, 256)
+        product = lax.dot_general(
+            att_ref[...],
+            weight_ref[block, :, columns],
+            (((1,), (1,)), ((), ())),
+            preferred_element_type=jnp.float32,
+        )
+        return fold(product)
+
+    for k, (dh, dx) in enumerate(ORDER):
+        first[k] = share(at(dh, dx, 1)).astype(jnp.bfloat16)
+        net.send(k, lambda k=k: first.at[k], lambda k=k: landed.at[k], sibling)
+
+    def summed(k):
+        dh, dx = ORDER[k]
+        own = share(at(dh, dx, 0))
+        net.arrive(k, lambda: landed.at[k], sibling)
+        return own + landed[k].astype(jnp.float32)
+
+    def pass_on(index, value, device):
+        second[index] = value.astype(jnp.bfloat16)
+        net.send(8 + index, lambda: second.at[index], lambda: ring.at[index], device)
+
+    def arrived(index, device):
+        net.arrive(8 + index, lambda: ring.at[index], device)
+        return ring[index].astype(jnp.float32)
+
+    pass_on(0, summed(0), before)
+    pass_on(1, summed(1), after)
+    pass_on(2, summed(2), after)
+    keep[0] = summed(3)
+    pass_on(4, keep[0] + arrived(0, after), before)
+    pass_on(3, summed(4), before)
+    keep[1] = summed(5)
+    pass_on(5, keep[1] + arrived(1, before), after)
+    keep[2] = summed(6)
+    mate_out[...] = (keep[2] + arrived(2, before) + arrived(4, after)).astype(jnp.bfloat16)
+    net.send(14, lambda: mate_out, lambda: mate_in, mate)
+    keep[3] = summed(7) + token_ref[...].astype(jnp.float32)
+    total = keep[3] + arrived(3, after) + arrived(5, before)
+    net.arrive(14, lambda: mate_in, mate)
+    out_ref[...] = (total + mate_in[...].astype(jnp.float32)).astype(jnp.bfloat16)
+    net.finish()
+
+
+def project_out(att, weights, tokens):
+    block = (FOLD, 128)
+    return pl.pallas_call(
+        out_kernel,
+        out_shape=jax.ShapeDtypeStruct(block, jnp.bfloat16),
+        in_specs=[vmem()] * 3,
+        out_specs=vmem(),
+        scratch_shapes=[
+            pltpu.VMEM((8,) + block, jnp.bfloat16),
+            pltpu.VMEM((8,) + block, jnp.bfloat16),
+            pltpu.VMEM((6,) + block, jnp.bfloat16),
+            pltpu.VMEM((6,) + block, jnp.bfloat16),
+            pltpu.VMEM((4,) + block, jnp.float32),
+            pltpu.VMEM(block, jnp.bfloat16),
+            pltpu.VMEM(block, jnp.bfloat16),
+            pltpu.SemaphoreType.DMA((16,)),
+            pltpu.SemaphoreType.DMA((16,)),
+        ],
+        compiler_params=pltpu.CompilerParams(
+            collective_id=2, has_side_effects=True, vmem_limit_bytes=40 * 1024 * 1024
+        ),
+    )(att, weights, tokens)
+
+
+def normed(token_rows, norm_gain, count):
     widened = token_rows.astype(jnp.float32)
-    inverse = lax.rsqrt(jnp.mean(widened * widened, axis=-1, keepdims=True) + 1e-05)
+    mean = jnp.sum(widened * widened, axis=-1, keepdims=True) * (1.0 / count)
+    inverse = lax.rsqrt(mean + 1e-05)
     return (widened * inverse * norm_gain.astype(jnp.float32)).astype(jnp.bfloat16)
 
 
@@ -35,8 +423,6 @@
     token_rows = jnp.concatenate(
         [prefill_hidden.reshape(prefill_count, col_width), decode_hidden], axis=0
     )
-    features = lax.all_gather(token_rows, "col", axis=1, tiled=True)
-    hidden = normed(features, norm_gain)
     heads_dev = query_weight.shape[1] // HD
     group_size = HQ // KV
     kv_dev = max(1, heads_dev // group_size)
@@ -47,26 +433,41 @@
     kv_columns = lax.dynamic_slice_in_dim(kv_weight, kv_first * HD, kv_dev * HD, 2).reshape(
         kv_weight.shape[0], 2 * kv_dev * HD
     )
-    query_full, kv_full = (
-        lax.all_gather(query_weight, "row", axis=0, tiled=True),
-        lax.all_gather(kv_columns, "row", axis=0, tiled=True),
-    )
-    query_sum = jnp.dot(hidden, query_full, preferred_element_type=jnp.float32)
-    kv_sum = jnp.dot(hidden, kv_full, preferred_element_type=jnp.float32)
+    weight_block = jnp.concatenate([query_weight, kv_columns, out_weight.T], axis=1)
+    weight_block = jnp.pad(weight_block, ((0, FEAT // 2 - weight_block.shape[0]), (0, 0)))
+    token_wide = jnp.pad(
+        token_rows.reshape(-1, 2, col_width // 2),
+        ((0, TOK - token_rows.shape[0]), (0, 0), (0, FEAT // 2 - col_width // 2)),
+    ).reshape(TOK, FEAT)
+    token_block = fold(token_wide)
+    all_weight, all_token = gather_first(weight_block, token_block)
+    weights = all_weight.reshape(4 * XN, FEAT, weight_block.shape[1])
+    features = unfold(all_token).transpose(1, 0, 2).reshape(TOK, 4 * XN * FEAT)
+    gain = jnp.pad(
+        norm_gain.reshape(-1, col_width // 2), ((0, 0), (0, FEAT // 2 - col_width // 2))
+    ).reshape(4 * XN * FEAT)
+    hidden = normed(features, gain, norm_gain.shape[0])
+    qkv_sum = jnp.dot(
+        hidden,
+        weights.reshape(4 * XN * FEAT, -1)[:, : heads_dev * HD + 2 * kv_dev * HD],
+        preferred_element_type=jnp.float32,
+    )[: prefill_count + decode_rows]
+    query_sum, kv_sum = qkv_sum[:, : heads_dev * HD], qkv_sum[:, heads_dev * HD :]
     queries = query_sum.astype(jnp.bfloat16)
     key_rows = kv_sum[:, : kv_dev * HD].astype(jnp.bfloat16)
     value_rows = kv_sum[:, kv_dev * HD :].astype(jnp.bfloat16)
     score_scale = 1.0 / math.sqrt(HD)
     sink_grid = sink_logits.astype(jnp.float32).reshape(kv_dev, per_kv)
     query_pre = queries[:prefill_count].reshape(spans, span_rows, kv_dev, per_kv, HD)
-    key_pre = key_rows[:prefill_count].reshape(spans, span_rows, kv_dev * HD)
-    value_pre = value_rows[:prefill_count].reshape(spans, span_rows, kv_dev * HD)
     positions = row_index * span_rows + jnp.arange(span_rows, dtype=jnp.int32)
     state_shape = (spans, kv_dev, per_kv, span_rows)
-    pieces = (
-        lax.all_gather(key_pre, "row", axis=1, tiled=True),
-        lax.all_gather(value_pre, "row", axis=1, tiled=True),
-    )
+    kv_all = (
+        gather_kv(kv_sum[:prefill_count].astype(jnp.bfloat16))
+        .reshape(-1, spans, span_rows, 2 * kv_dev * HD)
+        .transpose(1, 0, 2, 3)
+        .reshape(spans, -1, 2 * kv_dev * HD)
+    )
+    pieces = (kv_all[..., : kv_dev * HD], kv_all[..., kv_dev * HD :])
     running = jnp.broadcast_to(sink_grid[None, :, :, None], state_shape)
     denominator = jnp.ones(state_shape, jnp.float32)
     weighted = jnp.zeros(state_shape + (HD,), jnp.float32)
@@ -145,15 +546,13 @@
         .astype(jnp.bfloat16)
     )
     attended = jnp.concatenate([prefill_att, decode_att], axis=0)
-    partial_out = jnp.dot(
-        attended,
-        lax.all_gather(out_weight, "row", axis=1, tiled=True),
-        preferred_element_type=jnp.float32,
-    )
-    summed = lax.psum_scatter(
-        partial_out.astype(jnp.bfloat16), "col", scatter_dimension=1, tiled=True
-    ).astype(jnp.float32)
-    result = (token_rows.astype(jnp.float32) + summed).astype(jnp.bfloat16)
+    attended = jnp.pad(attended, ((0, TOK - attended.shape[0]), (0, 0)))
+    folded = project_out(attended, weights, token_block)
+    result = (
+        unfold(folded)
+        .reshape(TOK, 2, FEAT // 2)[: prefill_count + decode_rows, :, : col_width // 2]
+        .reshape(-1, col_width)
+    )
     return (result[:prefill_count].reshape(spans, span_rows, col_width), result[prefill_count:])
 
 

time: 1280 us -> 180 us (0.14)
  the two profiles are of different devices: /device:TPU:1 before, /device:TPU:2 now
where the time goes in v1:
time: 180 us
  Pallas kernels  128 us (71%)
  local copies, waits for them, and re-layouts  33.4 us (19%)
  matrix products  9.06 us (5%)
  other arithmetic  7.87 us (4%)
    pallas_call x1, Pallas kernels, gather_first(): pl.pallas_call(gather_kernel, out_shape=(jax.ShapeDtypeStruct((ZL * YN,)...  67.5 us
    pallas_call x1, Pallas kernels, gather_kv(): pl.pallas_call(kv_kernel, out_shape=jax.ShapeDtypeStruct((ZL * YN,) + blo...  34.4 us
    pallas_call x1, Pallas kernels, project_out(): pl.pallas_call(out_kernel, out_shape=jax.ShapeDtypeStruct(block, jnp.bflo...  26.7 us
    convert_element_type x2, local copies, waits for them, and re-layouts, normed(): widened = token_rows.astype(jnp.float32)  10.1 us
    reshape x1, local copies, waits for them, and re-layouts, body(): key_pool.reshape(pool_pages, page_len, KV, HD)  5.14 us
    dynamic_slice x1, local copies, waits for them, and re-layouts, body(): lax.dynamic_slice_in_dim(value_pool.reshape(pool_pages, page_len, KV, HD)...  4.48 us
    dot_general x1, matrix products, body(): jnp.dot(hidden, weights.reshape(4 * XN * FEAT, -1)[:, :heads_dev * HD + 2...  3.75 us

profile of v1, /device:TPU:2, one launch (start us, length us, event | category | flops | bytes accessed | tf_op | source)
XLA Modules:
  0.0 179.8 jit_solution(5295426782809870924)
XLA Ops:
  0.7 0.5 broadcast.156
  1.2 1.3 reduce.11
  2.5 0.7 convert_element_type.78
  3.2 0.7 iota_compare_fusion.4
  4.0 0.1 reshape.274
  4.1 0.8 concatenate.34
  4.9 0.8 reshape.254
  5.7 0.1 constant_dynamic-slice_fusion.2
  5.9 0.1 copy.28
  6.0 0.1 copy.29
  6.1 0.9 fusion.44.weight_ref
  7.0 0.1 iota_compare_fusion
  7.1 1.0 concatenate.33
  8.1 0.2 fusion.40
  8.4 0.1 reshape.253
  8.5 0.1 maximum_maximum_fusion.2.token_ref
  8.6 5.1 %reshape.260 = bf16[24,64,8,64]{3,2,1,0:T(8,128)(2,1)} reshape(bf16[24,64,512]{2,1,0:T(8,128)(2,1)} %param.18) | data formatting | bytes 3145728 | tf_op jit(solution)/shard_map/reshape | solution.py:508
  13.8 3.0 %reshape.263 = bf16[24,64,8,64]{3,2,1,0:T(8,128)(2,1)} reshape(bf16[24,64,512]{2,1,0:T(8,128)(2,1)S(1)} %copy-done.3) | data formatting | bytes 3145728 | tf_op jit(solution)/shard_map/reshape | solution.py:511
  16.8 4.5 %constant_dynamic-slice_fusion = (bf16[24,64,1,64]{3,2,1,0:T(2,128)(2,1)S(1)}, bf16[24,64,1,64]{3,2,1,0:T(2,128)(2,1)S(1)}) fusion(bf16[24,64,8,64]{3,2,1,0:T(8,128)(2,1)} %reshape.263, s32[]{:T(128)S(6)} %select_n.35, bf16[24,64,8,64]{3,2,1,0:T(8,128)(2,1)} %reshape.260), kind=kLoop, calls=%fused_computation.77 | loop fusion | bytes 786436 | tf_op jit(solution)/shard_map/dynamic_slice | solution.py:510
  21.3 0.6 gather_fusion.1
  22.0 0.6 gather_fusion
  22.6 67.5 %shard_map.122 = (bf16[32,96,640]{2,1,0:T(8,128)(2,1)S(1)}, bf16[16,408,128]{2,1,0:T(8,128)(2,1)S(1)}) custom-call(bf16[96,640]{1,0:T(8,128)(2,1)S(1)} %fusion.44.weight_ref, bf16[408,128]{1,0:T(8,128)(2,1)S(1)} %maximum_maximum_fusion.2.token_ref), custom_call_target="tpu_custom_call" | custom-call | tf_op jit(solution)/shard_map/pallas_call | solution.py:257
  90.2 0.2 fusion.57
  90.4 0.7 fusion.3
  91.1 0.5 convert_bitcast_fusion
  91.6 0.4 copy-done.1
  92.0 4.6 %copy.30 = f32[272,16,192]{2,1,0:T(8,128)} copy(f32[272,16,192]{2,0,1:T(8,128)S(1)} %convert_bitcast_fusion) | data formatting | bytes 6684672 | tf_op jit(solution)/shard_map/convert_element_type | solution.py:401
  96.6 5.4 %reshape.268 = f32[272,3072]{1,0:T(8,128)} reshape(f32[272,16,192]{2,1,0:T(8,128)} %copy.30) | data formatting | bytes 6684672 | tf_op jit(solution)/shard_map/convert_element_type | solution.py:401
  102.1 3.7 %fusion.16 = bf16[272,384]{1,0:T(8,128)(2,1)S(1)} fusion(bf16[3072,640]{1,0:T(8,128)(2,1)} %bitcast.90, f32[272,3072]{1,0:T(8,128)} %reshape.268, f32[3072]{0:T(1024)S(1)} %reshape.269, f32[272]{0:T(512)S(1)} %add_rsqrt_fusion), kind=kOutput, calls=%fused_computation.23 | convolution fusion | flops 644339712 | bytes 5923904 | tf_op jit(solution)/shard_map/dot_general | solution.py:450
  105.8 0.1 reshape.259
  105.9 0.3 fusion.60
  106.3 0.1 fusion.51
  106.4 0.2 fusion.45
  106.6 0.2 fusion.21
  107.0 0.2 reshape.257
  107.2 34.4 %shard_map.123 = bf16[32,256,128]{2,1,0:T(8,128)(2,1)S(1)} custom-call(bf16[256,128]{1,0:T(8,128)(2,1)S(1)} %slice.116.block_ref), custom_call_target="tpu_custom_call" | custom-call | tf_op jit(solution)/shard_map/pallas_call | solution.py:293
  141.5 0.2 copy.31
  141.7 1.5 fusion.2
  143.3 2.2 %fusion = f32[4,4,64]{2,1,0:T(4,128)S(1)} fusion(f32[4,2048,64,4]{1,2,3,0:T(8,128)S(1)} %get-tuple-element.21, f32[4,4,64]{2,1,0:T(4,128)S(1)} %broadcast_maximum_fusion, pred[64,2048]{1,0:T(8,128)(4,1)S(1)} %iota_compare_fusion), kind=kLoop, calls=%fused_computation.4 | loop fusion | flops 8387584 | bytes 8527872 | tf_op jit(solution)/shard_map/reduce_sum | solution.py:487
  145.6 3.1 %fusion.28 = bf16[4,64,1,4,64]{4,1,3,0,2:T(8,128)(2,1)S(1)} fusion(bf16[4,2048,128]{2,1,0:T(8,128)(2,1)S(1)} %bitcast.93, f32[4,2048,64,4]{1,2,3,0:T(8,128)S(1)} %get-tuple-element.21, f32[4,4,64]{2,1,0:T(4,128)S(1)} %broadcast_maximum_fusion, pred[64,2048]{1,0:T(8,128)(4,1)S(1)} %iota_compare_fusion, f32[4,4,64]{2,1,0:T(4,128)S(1)} %get-tuple-element.17, ...), kind=kOutput, calls=%fused_computation.31 | convolution fusion | flops 277020672 | bytes 10760192 | tf_op jit(solution)/shard_map/nkgqp,npkd->nkgqd/dot_general | solution.py:488
  148.7 0.2 copy.35
  148.9 0.2 convert_element_type.90
  149.2 2.1 %copy-done.2 = bf16[32,96,640]{2,1,0:T(8,128)(2,1)S(1)} copy-done((bf16[32,96,640]{2,1,0:T(8,128)(2,1)S(1)}, bf16[32,96,640]{2,1,0:T(8,128)(2,1)}, u32[]{:S(2)}) %copy-start.2) | copy-done | bytes 3932184
  151.3 26.7 %shard_map.124 = bf16[408,128]{1,0:T(8,128)(2,1)S(1)} custom-call(bf16[272,256]{1,0:T(8,128)(2,1)S(1)} %fusion.42.att_ref, bf16[16,192,640]{2,1,0:T(8,128)(2,1)S(1)} %bitcast.91, bf16[408,128]{1,0:T(8,128)(2,1)S(1)} %maximum_maximum_fusion.2.token_ref), custom_call_target="tpu_custom_call" | custom-call | tf_op jit(solution)/shard_map/pallas_call | solution.py:378
  178.1 0.1 reshape.266
  178.2 0.1 slice.123
  178.3 0.8 reshape.267
  179.1 0.7 slice.107
  (32 shorter events, 0.9 us)
Async XLA Ops:
  0.6 5.1 %copy-start = (bf16[90,2,512]{2,1,0:T(2,128)(2,1)S(1)}, bf16[90,2,512]{2,1,0:T(2,128)(2,1)}, u32[]{:S(2)}) copy-start(bf16[90,2,512]{2,1,0:T(2,128)(2,1)} %param.15) | copy-start | bytes 552964
  0.6 13.1 %copy-start.3 = (bf16[24,64,512]{2,1,0:T(8,128)(2,1)S(1)}, bf16[24,64,512]{2,1,0:T(8,128)(2,1)}, u32[]{:S(2)}) copy-start(bf16[24,64,512]{2,1,0:T(8,128)(2,1)} %param.19) | copy-start | bytes 4718596
  90.1 1.9 %copy-start.1 = (bf16[32,96,640]{2,1,0:T(8,128)(2,1)}, bf16[32,96,640]{2,1,0:T(8,128)(2,1)S(1)}, u32[]{:S(2)}) copy-start(bf16[32,96,640]{2,1,0:T(8,128)(2,1)S(1)} %get-tuple-element.5) | copy-start | bytes 11796484
  149.2 2.1 %copy-start.2 = (bf16[32,96,640]{2,1,0:T(8,128)(2,1)S(1)}, bf16[32,96,640]{2,1,0:T(8,128)(2,1)}, u32[]{:S(2)}) copy-start(bf16[32,96,640]{2,1,0:T(8,128)(2,1)} %copy-done.1) | copy-start | bytes 11796484

commit v2 on v1

--- a/solution.py
+++ b/solution.py
@@ -10,6 +10,7 @@
 HQ = 64
 KV = 8
 HD = 64
+WIDTH = 2880
 ZL = 8
 YN = 4
 XN = 4
@@ -19,6 +20,10 @@
 FEAT = 192
 MESH = pl.DeviceIdType.MESH
 ROW_COPIES = 64
+SHARED_COPIES = 128
+PIECE = FEAT // 2
+Q_AT, O_AT, KV_AT = 0, 2 * PIECE, 4 * PIECE
+BLOCK = 4 * PIECE + PIECE // 2
 COL_COPIES = 24
 
 
@@ -81,9 +86,11 @@
 
 
 class RowGather:
-    def __init__(self, block, out, send_sem, recv_sem):
+    def __init__(self, block, out, send_sem, recv_sem, other=None):
         row, col = lax.axis_index("row"), lax.axis_index("col")
         self.row = row
+        self.other = other
+        self.sibling = (row, col + 1 - 2 * lax.rem(col, 2))
         self.z, self.y = row // YN, lax.rem(row, YN)
         self.block, self.out = block, out
         self.up = (row + YN, col)
@@ -103,7 +110,11 @@
         ]
 
     def slot(self, z, shift):
-        return lambda: self.out.at[z * YN + lax.rem(self.y + shift + YN, YN)]
+        return lambda: self.out(z * YN + lax.rem(self.y + shift + YN, YN))
+
+    def share(self, index, src, z, shift, cond):
+        if self.other is not None:
+            self.net.send(64 + index, src, self.slot(z, shift), self.sibling, cond)
 
     def events(self, distance):
         events = [(0, self.z - distance, self.z - distance >= 0)]
@@ -131,6 +142,7 @@
             cond = None if distance == 0 else exists
             self.net.send(16 + way * 8 + distance, src, mine, self.after, cond)
             self.net.send(32 + way * 8 + distance, src, mine, self.before, cond)
+            self.share(way * 8 + distance, src, z, 0, cond)
 
     def along_y(self, distance):
         for way, z, exists in self.events(distance):
@@ -139,9 +151,11 @@
             self.net.arrive(16 + index, self.slot(z, -1), self.before, cond)
             if distance % 2 == 0:
                 self.net.send(48 + index, self.slot(z, -1), self.slot(z, -1), self.after, cond)
+            self.share(16 + index, self.slot(z, -1), z, -1, cond)
             self.net.arrive(32 + index, self.slot(z, 1), self.after, cond)
             if distance % 2 == 1:
                 self.net.send(48 + index, self.slot(z, 1), self.slot(z, 1), self.before, cond)
+            self.share(32 + index, self.slot(z, 1), z, 1, cond)
 
     def last(self):
         for distance in range(ZL):
@@ -149,6 +163,19 @@
                 cond = None if distance == 0 else exists
                 source = self.before if distance % 2 == 0 else self.after
                 self.net.arrive(48 + way * 8 + distance, self.slot(z, 2), source, cond)
+                self.share(48 + way * 8 + distance, self.slot(z, 2), z, 2, cond)
+        if self.other is not None:
+            for distance in range(ZL):
+                for way, z, exists in self.events(distance):
+                    cond = None if distance == 0 else exists
+                    for group, shift in enumerate((0, -1, 1, 2)):
+                        where = z * YN + lax.rem(self.y + shift + YN, YN)
+                        self.net.arrive(
+                            64 + group * 16 + way * 8 + distance,
+                            lambda where=where: self.other(where),
+                            self.sibling,
+                            cond,
+                        )
         self.net.finish()
 
 
@@ -209,10 +236,69 @@
         self.net.finish()
 
 
+def project(all_weight, hidden, query_ref, kv_ref, query_sum, kv_sum):
+    query_sum[...] = jnp.zeros_like(query_sum)
+    kv_sum[...] = jnp.zeros_like(kv_sum)
+
+    @pl.loop(0, 4 * XN)
+    def _(block):
+        def columns(first):
+            return jnp.concatenate(
+                [
+                    all_weight[2 * block, pl.ds(first, PIECE), :],
+                    all_weight[2 * block + 1, pl.ds(first, PIECE), :],
+                ],
+                axis=0,
+            )
+
+        def narrow(piece):
+            packed = all_weight[piece, pl.ds(KV_AT, PIECE // 2), :].astype(jnp.float32)
+            return jnp.concatenate([packed[:, :HD], packed[:, HD:]], axis=0)
+
+        mine = hidden[block]
+        for half in range(2):
+            query_sum[:, pl.ds(half * 128, 128)] += jnp.dot(
+                mine, columns(Q_AT + half * PIECE), preferred_element_type=jnp.float32
+            )
+        used = jnp.concatenate([narrow(2 * block), narrow(2 * block + 1)], axis=0)
+        kv_sum[...] += jnp.dot(
+            mine, used.astype(jnp.bfloat16), preferred_element_type=jnp.float32
+        )
+
+    query_ref[...] = query_sum[...].astype(jnp.bfloat16)
+    kv_ref[...] = jnp.concatenate([kv_sum[:HALF], kv_sum[HALF:]], axis=1).astype(jnp.bfloat16)
+
+
+def normalise(all_token, gain_ref, hidden, squares):
+    squares[...] = jnp.zeros_like(squares)
+
+    @pl.loop(0, 4 * XN)
+    def _(block):
+        wide = all_token[block].astype(jnp.float32)
+        squares[...] += wide * wide
+
+    tail = squares[TOK:]
+    tail = jnp.concatenate(
+        [
+            jnp.sum(tail[:, :64], axis=1, keepdims=True),
+            jnp.sum(tail[:, 64:], axis=1, keepdims=True),
+        ],
+        axis=0,
+    )
+    mean = (jnp.sum(squares[:TOK], axis=1, keepdims=True) + tail) * (1.0 / WIDTH)
+    inverse = lax.rsqrt(mean + 1e-05)
+
+    @pl.loop(0, 4 * XN)
+    def _(block):
+        rows = unfold(all_token[block].astype(jnp.float32))
+        hidden[block] = (rows * inverse * gain_ref[block]).astype(jnp.bfloat16)
+
+
 def gather_kernel(
-    weight_ref, token_ref, all_weight, all_token, rs, rr, cs, cr, local_sem
+    weight_ref, token_ref, gain_ref, all_weight, query_ref, kv_ref, all_token, hidden, squares,
+    query_sum, kv_sum, rs, rr, cs, cr, local_sem,
 ):
-    rows = RowGather(weight_ref, all_weight, rs, rr)
+    rows = RowGather(weight_ref, lambda index: all_weight.at[index], rs, rr)
     cols = ColGather(token_ref, all_token, cs, cr)
     greet(rows.partners() + cols.partners())
     cols.own(0)
@@ -242,27 +328,35 @@
     rows.along_y(5)
     rows.along_z(7)
     rows.along_y(6)
+    cols.last()
+    own_token.wait()
+    normalise(all_token, gain_ref, hidden, squares)
     rows.along_y(7)
-    cols.last()
     rows.last()
     own_weight.wait()
-    own_token.wait()
+    project(all_weight, hidden, query_ref, kv_ref, query_sum, kv_sum)
 
 
 def vmem():
     return pl.BlockSpec(memory_space=pltpu.VMEM)
 
 
-def gather_first(weight_block, token_block):
+def gather_first(weight_block, token_block, gain):
     return pl.pallas_call(
         gather_kernel,
         out_shape=(
             jax.ShapeDtypeStruct((ZL * YN,) + weight_block.shape, jnp.bfloat16),
-            jax.ShapeDtypeStruct((4 * XN,) + token_block.shape, jnp.bfloat16),
+            jax.ShapeDtypeStruct((TOK, 256), jnp.bfloat16),
+            jax.ShapeDtypeStruct((HALF, 128), jnp.bfloat16),
         ),
-        in_specs=[vmem()] * 2,
-        out_specs=(vmem(), vmem()),
+        in_specs=[vmem()] * 3,
+        out_specs=(vmem(),) * 3,
         scratch_shapes=[
+            pltpu.VMEM((4 * XN, FOLD, 128), jnp.bfloat16),
+            pltpu.VMEM((4 * XN, TOK, FEAT), jnp.bfloat16),
+            pltpu.VMEM((FOLD, 128), jnp.float32),
+            pltpu.VMEM((TOK, 256), jnp.float32),
+            pltpu.VMEM((TOK, HD), jnp.float32),
             pltpu.SemaphoreType.DMA((ROW_COPIES,)),
             pltpu.SemaphoreType.DMA((ROW_COPIES,)),
             pltpu.SemaphoreType.DMA((COL_COPIES,)),
@@ -272,14 +366,21 @@
         compiler_params=pltpu.CompilerParams(
             collective_id=0, has_side_effects=True, vmem_limit_bytes=40 * 1024 * 1024
         ),
-    )(weight_block, token_block)
+    )(weight_block, token_block, gain)
 
 
 def kv_kernel(block_ref, out_ref, send_sem, recv_sem, local_sem):
-    rows = RowGather(block_ref, out_ref, send_sem, recv_sem)
-    greet(rows.partners())
+    core = lax.rem(lax.axis_index("col"), 2)
+    rows = RowGather(
+        block_ref,
+        lambda index: out_ref.at[core, index],
+        send_sem,
+        recv_sem,
+        lambda index: out_ref.at[1 - core, index],
+    )
+    greet(rows.partners() + [(rows.sibling, None)])
     rows.along_z(0)
-    own = pltpu.make_async_copy(block_ref, out_ref.at[rows.row], local_sem.at[0])
+    own = pltpu.make_async_copy(block_ref, out_ref.at[core, rows.row], local_sem.at[0])
     own.start()
     for distance in range(1, ZL):
         rows.along_z(distance)
@@ -292,12 +393,12 @@
 def gather_kv(block):
     return pl.pallas_call(
         kv_kernel,
-        out_shape=jax.ShapeDtypeStruct((ZL * YN,) + block.shape, jnp.bfloat16),
+        out_shape=jax.ShapeDtypeStruct((2, ZL * YN) + block.shape, jnp.bfloat16),
         in_specs=[vmem()],
         out_specs=vmem(),
         scratch_shapes=[
-            pltpu.SemaphoreType.DMA((ROW_COPIES,)),
-            pltpu.SemaphoreType.DMA((ROW_COPIES,)),
+            pltpu.SemaphoreType.DMA((SHARED_COPIES,)),
+            pltpu.SemaphoreType.DMA((SHARED_COPIES,)),
             pltpu.SemaphoreType.DMA((1,)),
         ],
         compiler_params=pltpu.CompilerParams(
@@ -328,13 +429,21 @@
     net = Sender(send_sem, recv_sem)
 
     def share(block):
-        columns = pl.ds(384, 256)
-        product = lax.dot_general(
-            att_ref[...],
-            weight_ref[block, :, columns],
-            (((1,), (1,)), ((), ())),
-            preferred_element_type=jnp.float32,
-        )
+        product = jnp.zeros((TOK, FEAT), jnp.float32)
+        for half in range(2):
+            columns = jnp.concatenate(
+                [
+                    weight_ref[2 * block + piece, pl.ds(O_AT + half * PIECE, PIECE), :]
+                    for piece in range(2)
+                ],
+                axis=0,
+            )
+            product += lax.dot_general(
+                att_ref[:, pl.ds(half * 128, 128)],
+                columns,
+                (((1,), (1,)), ((), ())),
+                preferred_element_type=jnp.float32,
+            )
         return fold(product)
 
     for k, (dh, dx) in enumerate(ORDER):
@@ -397,13 +506,6 @@
     )(att, weights, tokens)
 
 
-def normed(token_rows, norm_gain, count):
-    widened = token_rows.astype(jnp.float32)
-    mean = jnp.sum(widened * widened, axis=-1, keepdims=True) * (1.0 / count)
-    inverse = lax.rsqrt(mean + 1e-05)
-    return (widened * inverse * norm_gain.astype(jnp.float32)).astype(jnp.bfloat16)
-
-
 def body(
     prefill_hidden,
     decode_hidden,
@@ -419,118 +521,130 @@
 ):
     spans, span_rows, col_width = prefill_hidden.shape
     decode_rows = decode_hidden.shape[0]
-    prefill_count = spans * span_rows
-    token_rows = jnp.concatenate(
-        [prefill_hidden.reshape(prefill_count, col_width), decode_hidden], axis=0
-    )
-    heads_dev = query_weight.shape[1] // HD
-    group_size = HQ // KV
-    kv_dev = max(1, heads_dev // group_size)
-    per_kv = heads_dev // kv_dev
+    heads = query_weight.shape[1] // HD
     col_index = lax.axis_index("col")
     row_index = lax.axis_index("row")
-    kv_first = col_index * heads_dev // group_size
-    kv_columns = lax.dynamic_slice_in_dim(kv_weight, kv_first * HD, kv_dev * HD, 2).reshape(
-        kv_weight.shape[0], 2 * kv_dev * HD
-    )
-    weight_block = jnp.concatenate([query_weight, kv_columns, out_weight.T], axis=1)
-    weight_block = jnp.pad(weight_block, ((0, FEAT // 2 - weight_block.shape[0]), (0, 0)))
-    token_wide = jnp.pad(
-        token_rows.reshape(-1, 2, col_width // 2),
-        ((0, TOK - token_rows.shape[0]), (0, 0), (0, FEAT // 2 - col_width // 2)),
-    ).reshape(TOK, FEAT)
-    token_block = fold(token_wide)
-    all_weight, all_token = gather_first(weight_block, token_block)
-    weights = all_weight.reshape(4 * XN, FEAT, weight_block.shape[1])
-    features = unfold(all_token).transpose(1, 0, 2).reshape(TOK, 4 * XN * FEAT)
-    gain = jnp.pad(
-        norm_gain.reshape(-1, col_width // 2), ((0, 0), (0, FEAT // 2 - col_width // 2))
-    ).reshape(4 * XN * FEAT)
-    hidden = normed(features, gain, norm_gain.shape[0])
-    qkv_sum = jnp.dot(
-        hidden,
-        weights.reshape(4 * XN * FEAT, -1)[:, : heads_dev * HD + 2 * kv_dev * HD],
+    core = col_index % 2
+    kv_head = col_index * heads // (HQ // KV)
+    half_rows = (spans // 2) * span_rows
+    gap = HALF - half_rows - decode_rows
+
+    def padded(array, axis):
+        pads = [(0, 0)] * array.ndim
+        pads[axis] = (0, PIECE - array.shape[axis])
+        return jnp.pad(array, pads)
+
+    def two_halves(prefill, decode):
+        wide = prefill.shape[1]
+        return jnp.concatenate(
+            [
+                prefill[:half_rows],
+                decode,
+                jnp.zeros((gap, wide), decode.dtype),
+                prefill[half_rows:],
+                jnp.zeros((HALF - half_rows, wide), decode.dtype),
+            ],
+            axis=0,
+        )
+
+    kv_mine = padded(
+        lax.dynamic_slice(
+            kv_weight, (0, core, kv_head * HD), (kv_weight.shape[0], 1, HD)
+        ).reshape(-1, HD),
+        0,
+    )
+    query_mine = padded(query_weight, 0)
+    out_mine = padded(out_weight.T, 0)
+    weight_block = jnp.concatenate(
+        [
+            query_mine[:, :128],
+            query_mine[:, 128:],
+            out_mine[:, :128],
+            out_mine[:, 128:],
+            jnp.concatenate([kv_mine[: PIECE // 2], kv_mine[PIECE // 2 :]], axis=1),
+        ],
+        axis=0,
+    )
+    part = col_width // 2
+    token_rows = two_halves(prefill_hidden.reshape(-1, col_width), decode_hidden)
+    token_block = fold(
+        jnp.concatenate(
+            [padded(token_rows[:, :part], 1), padded(token_rows[:, part:], 1)], axis=1
+        )
+    )
+    gain = (
+        padded(norm_gain.astype(jnp.float32).reshape(-1, part), 1).reshape(4 * XN, 1, FEAT)
+    )
+    all_weight, queries, kv_block = gather_first(weight_block, token_block, gain)
+    kv_all = gather_kv(kv_block)
+    score_scale = 1.0 / math.sqrt(HD)
+    sink = sink_logits.astype(jnp.float32)
+    query_pre = jnp.concatenate(
+        [queries[:half_rows], queries[HALF : HALF + half_rows]], axis=0
+    ).reshape(spans, span_rows, heads, HD)
+    key_pair, value_pair = [
+        jnp.concatenate(
+            [
+                kv_all[which, :, :half_rows, side * HD : (side + 1) * HD]
+                .reshape(-1, spans // 2, span_rows, HD)
+                .transpose(1, 0, 2, 3)
+                .reshape(spans // 2, -1, HD)
+                for side in range(2)
+            ],
+            axis=0,
+        )
+        for which in range(2)
+    ]
+    positions = row_index * span_rows + jnp.arange(span_rows, dtype=jnp.int32)
+    scores = (
+        jnp.einsum("sqgd,spd->sgqp", query_pre, key_pair, preferred_element_type=jnp.float32)
+        * score_scale
+    )
+    key_pos = jnp.arange(key_pair.shape[1], dtype=jnp.int32)
+    scores = jnp.where(key_pos[None, :] <= positions[:, None], scores, -jnp.inf)
+    sink_pre = sink[None, :, None]
+    highest = jnp.maximum(jnp.max(scores, axis=-1), sink_pre)
+    probs = jnp.exp(scores - highest[..., None])
+    denominator = jnp.sum(probs, axis=-1) + jnp.exp(sink_pre - highest)
+    weighted = jnp.einsum(
+        "sgqp,spd->sgqd",
+        probs.astype(jnp.bfloat16),
+        value_pair,
         preferred_element_type=jnp.float32,
-    )[: prefill_count + decode_rows]
-    query_sum, kv_sum = qkv_sum[:, : heads_dev * HD], qkv_sum[:, heads_dev * HD :]
-    queries = query_sum.astype(jnp.bfloat16)
-    key_rows = kv_sum[:, : kv_dev * HD].astype(jnp.bfloat16)
-    value_rows = kv_sum[:, kv_dev * HD :].astype(jnp.bfloat16)
-    score_scale = 1.0 / math.sqrt(HD)
-    sink_grid = sink_logits.astype(jnp.float32).reshape(kv_dev, per_kv)
-    query_pre = queries[:prefill_count].reshape(spans, span_rows, kv_dev, per_kv, HD)
-    positions = row_index * span_rows + jnp.arange(span_rows, dtype=jnp.int32)
-    state_shape = (spans, kv_dev, per_kv, span_rows)
-    kv_all = (
-        gather_kv(kv_sum[:prefill_count].astype(jnp.bfloat16))
-        .reshape(-1, spans, span_rows, 2 * kv_dev * HD)
-        .transpose(1, 0, 2, 3)
-        .reshape(spans, -1, 2 * kv_dev * HD)
-    )
-    pieces = (kv_all[..., : kv_dev * HD], kv_all[..., kv_dev * HD :])
-    running = jnp.broadcast_to(sink_grid[None, :, :, None], state_shape)
-    denominator = jnp.ones(state_shape, jnp.float32)
-    weighted = jnp.zeros(state_shape + (HD,), jnp.float32)
-    piece_len = pieces[0].shape[1]
-    key_piece = pieces[0].reshape(spans, piece_len, kv_dev, HD)
-    value_piece = pieces[1].reshape(spans, piece_len, kv_dev, HD)
-    scores = (
-        jnp.einsum("nqkgd,npkd->nkgqp", query_pre, key_piece, preferred_element_type=jnp.float32)
-        * score_scale
-    )
-    key_pos = jnp.arange(piece_len, dtype=jnp.int32)
-    allowed = key_pos[None, :] <= positions[:, None]
-    scores = jnp.where(allowed, scores, -jnp.inf)
-    newest = jnp.maximum(running, jnp.max(scores, axis=-1))
-    probs_soft = jnp.exp(scores - newest[..., None])
-    factor = jnp.exp(running - newest)
-    denominator = denominator * factor + jnp.sum(probs_soft, axis=-1)
-    weighted = weighted * factor[..., None] + jnp.einsum(
-        "nkgqp,npkd->nkgqd",
-        probs_soft.astype(jnp.bfloat16),
-        value_piece,
-        preferred_element_type=jnp.float32,
-    )
-    running, denominator, weighted = (newest, denominator, weighted)
+    )
     prefill_att = (
         (weighted / denominator[..., None])
-        .transpose(0, 3, 1, 2, 4)
-        .reshape(prefill_count, heads_dev * HD)
+        .transpose(0, 2, 1, 3)
+        .reshape(spans * span_rows, heads * HD)
         .astype(jnp.bfloat16)
     )
-    query_dec = queries[prefill_count:].reshape(decode_rows, kv_dev, per_kv, HD)
-    key_new = key_rows[prefill_count:].reshape(decode_rows, kv_dev, HD)
-    value_new = value_rows[prefill_count:].reshape(decode_rows, kv_dev, HD)
-    pool_pages, page_len, pool_width = key_pool.shape
+    query_dec = queries[half_rows : half_rows + decode_rows].reshape(decode_rows, heads, HD)
+    new_rows = lax.dynamic_index_in_dim(kv_all, row_index, 1, keepdims=False)
+    key_new = new_rows[0, half_rows : half_rows + decode_rows, :HD]
+    value_new = new_rows[1, half_rows : half_rows + decode_rows, :HD]
     table = page_table.reshape(decode_rows, -1)
-    max_pages = table.shape[1]
-    key_mine = lax.dynamic_slice_in_dim(
-        key_pool.reshape(pool_pages, page_len, KV, HD), kv_first, kv_dev, 2
-    )
-    value_mine = lax.dynamic_slice_in_dim(
-        value_pool.reshape(pool_pages, page_len, KV, HD), kv_first, kv_dev, 2
-    )
-    key_cache = key_mine[table].reshape(decode_rows, max_pages * page_len, kv_dev, HD)
-    value_cache = value_mine[table].reshape(decode_rows, max_pages * page_len, kv_dev, HD)
+    page_len = key_pool.shape[1]
+    key_mine = lax.dynamic_slice_in_dim(key_pool, kv_head * HD, HD, 2)
+    value_mine = lax.dynamic_slice_in_dim(value_pool, kv_head * HD, HD, 2)
+    cached = table.shape[1] * page_len
+    key_cache = key_mine[table].reshape(decode_rows, cached, HD)
+    value_cache = value_mine[table].reshape(decode_rows, cached, HD)
     cache_scores = (
-        jnp.einsum("skgd,stkd->skgt", query_dec, key_cache, preferred_element_type=jnp.float32)
+        jnp.einsum("sgd,std->sgt", query_dec, key_cache, preferred_element_type=jnp.float32)
         * score_scale
     )
-    live = (
-        jnp.arange(max_pages * page_len, dtype=jnp.int32)[None, :]
-        < lengths.reshape(decode_rows)[:, None]
-    )
-    cache_scores = jnp.where(live[:, None, None, :], cache_scores, -jnp.inf)
+    live = jnp.arange(cached, dtype=jnp.int32)[None, :] < lengths.reshape(decode_rows)[:, None]
+    cache_scores = jnp.where(live[:, None, :], cache_scores, -jnp.inf)
     self_scores = (
-        jnp.einsum("skgd,skd->skg", query_dec, key_new, preferred_element_type=jnp.float32)
+        jnp.einsum("sgd,sd->sg", query_dec, key_new, preferred_element_type=jnp.float32)
         * score_scale
     )
-    highest = jnp.maximum(jnp.maximum(jnp.max(cache_scores, axis=-1), self_scores), sink_grid[None])
+    highest = jnp.maximum(jnp.maximum(jnp.max(cache_scores, axis=-1), self_scores), sink[None])
     cache_probs = jnp.exp(cache_scores - highest[..., None])
     self_probs = jnp.exp(self_scores - highest)
-    denom_dec = jnp.sum(cache_probs, axis=-1) + self_probs + jnp.exp(sink_grid[None] - highest)
+    denom_dec = jnp.sum(cache_probs, axis=-1) + self_probs + jnp.exp(sink[None] - highest)
     decode_sum = jnp.einsum(
-        "skgt,stkd->skgd",
+        "sgt,std->sgd",
         cache_probs.astype(jnp.bfloat16),
         value_cache,
         preferred_element_type=jnp.float32,
@@ -538,22 +652,18 @@
     decode_sum = (
         decode_sum
         + self_probs.astype(jnp.bfloat16).astype(jnp.float32)[..., None]
-        * value_new.astype(jnp.float32)[:, :, None, :]
+        * value_new.astype(jnp.float32)[:, None, :]
     )
     decode_att = (
-        (decode_sum / denom_dec[..., None])
-        .reshape(decode_rows, heads_dev * HD)
-        .astype(jnp.bfloat16)
-    )
-    attended = jnp.concatenate([prefill_att, decode_att], axis=0)
-    attended = jnp.pad(attended, ((0, TOK - attended.shape[0]), (0, 0)))
-    folded = project_out(attended, weights, token_block)
-    result = (
-        unfold(folded)
-        .reshape(TOK, 2, FEAT // 2)[: prefill_count + decode_rows, :, : col_width // 2]
-        .reshape(-1, col_width)
-    )
-    return (result[:prefill_count].reshape(spans, span_rows, col_width), result[prefill_count:])
+        (decode_sum / denom_dec[..., None]).reshape(decode_rows, heads * HD).astype(jnp.bfloat16)
+    )
+    result = unfold(project_out(two_halves(prefill_att, decode_att), all_weight, token_block))
+    result = jnp.concatenate([result[:, :part], result[:, PIECE : PIECE + part]], axis=1)
+    prefill_out = jnp.concatenate([result[:half_rows], result[HALF : HALF + half_rows]], axis=0)
+    return (
+        prefill_out.reshape(spans, span_rows, col_width),
+        result[half_rows : half_rows + decode_rows],
+    )
 
 
 def solution(mesh):

time: 180 us -> 177 us (0.983)
  matrix products: 9.06 us -> 5.21 us
  Pallas kernels: 128 us -> 131 us
    convert_element_type x6 -> x1, local copies, waits for them, and re-layouts: 10.6 us -> 0.08 us  [body(): (decode_sum / denom_dec[..., None]).reshape(decode_rows, heads * HD)]
    transpose x0 -> x4, local copies, waits for them, and re-layouts: none -> 9.53 us  [body(): key_pair, value_pair = [jnp.concatenate([kv_all[which, :, :half_rows, sid...]
    reshape x8, local copies, waits for them, and re-layouts: 10.3 us -> 6.03 us  [the longest x4 4.88 us: body(): key_pair, value_pair = [jnp.concatenate([kv_all[which, :, :half_rows, sid...]
    unnamed x11 -> x17, local copies, waits for them, and re-layouts: 3.14 us -> 7.28 us
    slice x7 -> x15, local copies, waits for them, and re-layouts: 0.79 us -> 4.9 us  [the longest x1 2.77 us: body(): kv_all[which, :, :half_rows, side * HD:(side + 1) * HD]]
    dot_general x6 -> x5, matrix products: 9.06 us -> 5.21 us  [the longest x1 2.6 us: body(): jnp.einsum('sqgd,spd->sgqp', query_pre, key_pair, preferred_element_type=...]
    dynamic_slice x3 -> x2, local copies, waits for them, and re-layouts: 4.71 us -> 1.56 us  [the longest x1 1.42 us: body(): value_mine = lax.dynamic_slice_in_dim(value_pool, kv_head * HD, HD, 2)]
where the time goes in v2:
time: 177 us; the launch traced here: 176 us
  Pallas kernels  131 us (74%)
  local copies, waits for them, and re-layouts  31.8 us (18%)
  other arithmetic  7.27 us (4%)
  matrix products  5.21 us (3%)
    pallas_call x1, Pallas kernels, gather_first(): pl.pallas_call(gather_kernel, out_shape=(jax.ShapeDtypeStruct((ZL * YN,)...  69.1 us
    pallas_call x1, Pallas kernels, gather_kv(): pl.pallas_call(kv_kernel, out_shape=jax.ShapeDtypeStruct((2, ZL * YN) + b...  34 us
    pallas_call x1, Pallas kernels, project_out(): pl.pallas_call(out_kernel, out_shape=jax.ShapeDtypeStruct(block, jnp.bflo...  27.9 us
    transpose x4, local copies, waits for them, and re-layouts, body(): key_pair, value_pair = [jnp.concatenate([kv_all[which, :, :half_rows, sid...  9.53 us
    unnamed x17, local copies, waits for them, and re-layouts  7.28 us
    reshape x4, local copies, waits for them, and re-layouts, body(): key_pair, value_pair = [jnp.concatenate([kv_all[which, :, :half_rows, sid...  4.88 us

profile of v2, /device:TPU:2, one launch (start us, length us, event | category | flops | bytes accessed | tf_op | source)
XLA Modules:
  0.0 176.3 jit_solution(13370453289759732536)
XLA Ops:
  0.7 0.5 broadcast.100
  1.2 1.3 reduce.3
  2.5 0.7 convert_element_type.46
  3.2 0.7 iota_compare_fusion.2
  4.1 0.8 reshape.131
  5.0 0.1 constant_dynamic-slice_fusion.2
  5.2 0.7 fusion.28
  6.0 0.8 fusion.29
  6.7 0.8 fusion.30
  7.5 0.8 fusion.31
  8.3 0.1 iota_compare_fusion
  8.4 0.9 fusion.49
  9.3 0.7 concatenate.44
  10.2 0.7 slice_select_fusion
  10.9 0.1 pad_slice_fusion.6
  10.9 0.1 fusion.27.token_ref
  11.1 1.4 constant_dynamic-slice_fusion
  12.5 0.6 gather_fusion.1
  13.1 0.6 gather_fusion
  13.7 69.1 %shard_map.122 = (bf16[32,432,128]{2,1,0:T(8,128)(2,1)S(1)}, bf16[272,256]{1,0:T(8,128)(2,1)S(1)}, bf16[136,128]{1,0:T(8,128)(2,1)S(1)}) custom-call(bf16[432,128]{1,0:T(8,128)(2,1)S(1)} %maximum_dynamic-update-slice_fusion.weight_ref, bf16[408,128]{1,0:T(8,128)(2,1)S(1)} %fusion.27.token_ref, f32[16,1,192]{2,1,0:T(1,128)S(1)} %reshape.145.gain_ref), custom_call_target="tpu_custom_call" | custom-call | tf_op jit(solution)/shard_map/pallas_call | solution.py:345
  82.9 1.7 copy-done.1
  84.7 0.3 fusion.51
  85.0 0.2 reshape.136
  85.2 34.0 %shard_map.123 = bf16[2,32,136,128]{3,2,1,0:T(8,128)(2,1)S(1)} custom-call(bf16[136,128]{1,0:T(8,128)(2,1)S(1)} %get-tuple-element.5.block_ref), custom_call_target="tpu_custom_call" | custom-call | tf_op jit(solution)/shard_map/pallas_call | solution.py:394
  119.3 0.1 fusion.36
  119.4 0.2 fusion.32
  119.6 0.2 fusion.11
  119.9 2.8 %fusion.45 = (bf16[1,32,128,64]{3,2,1,0:T(8,128)(2,1)}, bf16[1,32,128,64]{3,2,1,0:T(8,128)(2,1)}, bf16[1,32,128,64]{3,2,1,0:T(8,128)(2,1)}, bf16[1,32,128,64]{3,2,1,0:T(8,128)(2,1)}) fusion(bf16[2,32,136,128]{3,2,1,0:T(8,128)(2,1)S(1)} %shard_map.123), kind=kLoop, calls=%fused_computation.78 | loop fusion | bytes 4194304 | tf_op jit(solution)/shard_map/slice | solution.py:588
  122.7 2.7 %copy.14 = bf16[2,32,64,64]{2,1,3,0:T(8,128)(2,1)S(1)} copy(bf16[2,32,64,64]{3,2,0,1:T(8,128)(2,1)} %bitcast.100) | data formatting | bytes 1048576 | tf_op jit(solution)/shard_map/transpose | solution.py:590
  125.4 1.6 reshape.134
  127.0 2.6 %copy.18 = bf16[2,32,64,64]{2,1,3,0:T(8,128)(2,1)S(1)} copy(bf16[2,32,64,64]{3,2,0,1:T(8,128)(2,1)} %bitcast.99) | data formatting | bytes 1048576 | tf_op jit(solution)/shard_map/transpose | solution.py:590
  129.6 0.8 reshape.138
  130.5 2.6 %copy.17 = bf16[2,32,64,64]{2,1,3,0:T(8,128)(2,1)S(1)} copy(bf16[2,32,64,64]{3,2,0,1:T(8,128)(2,1)} %bitcast.98) | data formatting | bytes 1048576 | tf_op jit(solution)/shard_map/transpose | solution.py:590
  133.1 1.6 reshape.137
  134.7 1.6 copy.15
  136.3 0.8 reshape.135
  137.2 2.6 %fusion.2 = (f32[4,4,64]{2,1,0:T(4,128)S(1)}, f32[4,2048,64,4]{1,2,3,0:T(8,128)S(1)}) fusion(pred[64,2048]{1,0:T(8,128)(4,1)S(1)} %iota_compare_fusion, bf16[4,64,4,64]{3,2,1,0:T(4,128)(2,1)S(1)} %reshape.136, bf16[2,2048,64]{1,2,0:T(8,128)(2,1)S(1)} %reshape.135, bf16[2,2048,64]{1,2,0:T(8,128)(2,1)} %reshape.134), kind=kOutput, calls=%fused_computation.6 | convolution fusion | flops 276823040 | bytes 9703424 | tf_op jit(solution)/shard_map/sqgd,spd->sgqp/dot_general | solution.py:600
  139.9 2.4 %fusion = f32[4,4,64]{2,1,0:T(4,128)S(1)} fusion(f32[4,2048,64,4]{1,2,3,0:T(8,128)S(1)} %get-tuple-element.29, f32[4,4,64]{2,1,0:T(4,128)S(1)} %broadcast_maximum_fusion, pred[64,2048]{1,0:T(8,128)(4,1)S(1)} %iota_compare_fusion), kind=kLoop, calls=%fused_computation.4 | loop fusion | flops 8387584 | bytes 8527872 | tf_op jit(solution)/shard_map/reduce_sum | solution.py:608
  142.3 1.9 %fusion.20 = bf16[4,64,4,64]{3,1,2,0:T(8,128)(2,1)S(1)} fusion(bf16[2,2048,64]{1,2,0:T(8,128)(2,1)S(1)} %reshape.138, bf16[2,2048,64]{1,2,0:T(8,128)(2,1)S(1)} %copy-done.4, f32[4,2048,64,4]{1,2,3,0:T(8,128)S(1)} %get-tuple-element.29, f32[4,4,64]{2,1,0:T(4,128)S(1)} %broadcast_maximum_fusion, pred[64,2048]{1,0:T(8,128)(4,1)S(1)} %iota_compare_fusion, ...), kind=kOutput, calls=%fused_computation.23 | convolution fusion | flops 277479424 | bytes 9707520 | tf_op jit(solution)/shard_map/sgqp,spd->sgqd/dot_general | solution.py:609
  144.3 0.1 copy.22
  144.4 0.1 slice.145
  144.6 0.1 copy.19
  144.7 0.1 slice.140
  144.9 2.0 %copy-done.2 = bf16[32,432,128]{2,1,0:T(8,128)(2,1)S(1)} copy-done((bf16[32,432,128]{2,1,0:T(8,128)(2,1)S(1)}, bf16[32,432,128]{2,1,0:T(8,128)(2,1)}, u32[]{:S(2)}) %copy-start.2) | copy-done | bytes 3538968
  146.9 27.9 %shard_map.124 = bf16[408,128]{1,0:T(8,128)(2,1)S(1)} custom-call(bf16[272,256]{1,0:T(8,128)(2,1)S(1)} %concatenate.51.att_ref, bf16[32,432,128]{2,1,0:T(8,128)(2,1)S(1)} %copy-done.2, bf16[408,128]{1,0:T(8,128)(2,1)S(1)} %fusion.27.token_ref), custom_call_target="tpu_custom_call" | custom-call | tf_op jit(solution)/shard_map/pallas_call | solution.py:487
  174.9 0.1 fusion.26
  175.0 0.6 slice.167
  175.6 0.7 pad_maximum_fusion.2
  (43 shorter events, 1.1 us)
Async XLA Ops:
  0.6 4.4 %copy-start = (bf16[90,2,512]{2,1,0:T(2,128)(2,1)S(1)}, bf16[90,2,512]{2,1,0:T(2,128)(2,1)}, u32[]{:S(2)}) copy-start(bf16[90,2,512]{2,1,0:T(2,128)(2,1)} %param.15) | copy-start | bytes 552964
  82.9 1.7 copy-start.1
  122.7 12.0 %copy-start.3 = (bf16[1,32,128,64]{3,2,1,0:T(8,128)(2,1)S(1)}, bf16[1,32,128,64]{3,2,1,0:T(8,128)(2,1)}, u32[]{:S(2)}) copy-start(bf16[1,32,128,64]{3,2,1,0:T(8,128)(2,1)} %get-tuple-element.13) | copy-start | bytes 1572868
  137.2 5.2 %copy-start.4 = (bf16[2,2048,64]{1,2,0:T(8,128)(2,1)S(1)}, bf16[2,2048,64]{1,2,0:T(8,128)(2,1)}, u32[]{:S(2)}) copy-start(bf16[2,2048,64]{1,2,0:T(8,128)(2,1)} %reshape.137) | copy-start | bytes 1572868
  144.9 2.0 %copy-start.2 = (bf16[32,432,128]{2,1,0:T(8,128)(2,1)S(1)}, bf16[32,432,128]{2,1,0:T(8,128)(2,1)}, u32[]{:S(2)}) copy-start(bf16[32,432,128]{2,1,0:T(8,128)(2,1)} %copy-done.1) | copy-start | bytes 10616836

commit v3 on v2

--- a/solution.py
+++ b/solution.py
@@ -20,10 +20,8 @@
 FEAT = 192
 MESH = pl.DeviceIdType.MESH
 ROW_COPIES = 64
-SHARED_COPIES = 128
 PIECE = FEAT // 2
 Q_AT, O_AT, KV_AT = 0, 2 * PIECE, 4 * PIECE
-BLOCK = 4 * PIECE + PIECE // 2
 COL_COPIES = 24
 
 
@@ -86,11 +84,9 @@
 
 
 class RowGather:
-    def __init__(self, block, out, send_sem, recv_sem, other=None):
+    def __init__(self, block, out, send_sem, recv_sem):
         row, col = lax.axis_index("row"), lax.axis_index("col")
         self.row = row
-        self.other = other
-        self.sibling = (row, col + 1 - 2 * lax.rem(col, 2))
         self.z, self.y = row // YN, lax.rem(row, YN)
         self.block, self.out = block, out
         self.up = (row + YN, col)
@@ -111,10 +107,6 @@
 
     def slot(self, z, shift):
         return lambda: self.out(z * YN + lax.rem(self.y + shift + YN, YN))
-
-    def share(self, index, src, z, shift, cond):
-        if self.other is not None:
-            self.net.send(64 + index, src, self.slot(z, shift), self.sibling, cond)
 
     def events(self, distance):
         events = [(0, self.z - distance, self.z - distance >= 0)]
@@ -142,7 +134,6 @@
             cond = None if distance == 0 else exists
             self.net.send(16 + way * 8 + distance, src, mine, self.after, cond)
             self.net.send(32 + way * 8 + distance, src, mine, self.before, cond)
-            self.share(way * 8 + distance, src, z, 0, cond)
 
     def along_y(self, distance):
         for way, z, exists in self.events(distance):
@@ -151,11 +142,9 @@
             self.net.arrive(16 + index, self.slot(z, -1), self.before, cond)
             if distance % 2 == 0:
                 self.net.send(48 + index, self.slot(z, -1), self.slot(z, -1), self.after, cond)
-            self.share(16 + index, self.slot(z, -1), z, -1, cond)
             self.net.arrive(32 + index, self.slot(z, 1), self.after, cond)
             if distance % 2 == 1:
                 self.net.send(48 + index, self.slot(z, 1), self.slot(z, 1), self.before, cond)
-            self.share(32 + index, self.slot(z, 1), z, 1, cond)
 
     def last(self):
         for distance in range(ZL):
@@ -163,19 +152,6 @@
                 cond = None if distance == 0 else exists
                 source = self.before if distance % 2 == 0 else self.after
                 self.net.arrive(48 + way * 8 + distance, self.slot(z, 2), source, cond)
-                self.share(48 + way * 8 + distance, self.slot(z, 2), z, 2, cond)
-        if self.other is not None:
-            for distance in range(ZL):
-                for way, z, exists in self.events(distance):
-                    cond = None if distance == 0 else exists
-                    for group, shift in enumerate((0, -1, 1, 2)):
-                        where = z * YN + lax.rem(self.y + shift + YN, YN)
-                        self.net.arrive(
-                            64 + group * 16 + way * 8 + distance,
-                            lambda where=where: self.other(where),
-                            self.sibling,
-                            cond,
-                        )
         self.net.finish()
 
 
@@ -251,22 +227,15 @@
                 axis=0,
             )
 
-        def narrow(piece):
-            packed = all_weight[piece, pl.ds(KV_AT, PIECE // 2), :].astype(jnp.float32)
-            return jnp.concatenate([packed[:, :HD], packed[:, HD:]], axis=0)
-
         mine = hidden[block]
         for half in range(2):
             query_sum[:, pl.ds(half * 128, 128)] += jnp.dot(
                 mine, columns(Q_AT + half * PIECE), preferred_element_type=jnp.float32
             )
-        used = jnp.concatenate([narrow(2 * block), narrow(2 * block + 1)], axis=0)
-        kv_sum[...] += jnp.dot(
-            mine, used.astype(jnp.bfloat16), preferred_element_type=jnp.float32
-        )
+        kv_sum[...] += jnp.dot(mine, columns(KV_AT), preferred_element_type=jnp.float32)
 
     query_ref[...] = query_sum[...].astype(jnp.bfloat16)
-    kv_ref[...] = jnp.concatenate([kv_sum[:HALF], kv_sum[HALF:]], axis=1).astype(jnp.bfloat16)
+    kv_ref[...] = kv_sum[...].astype(jnp.bfloat16)
 
 
 def normalise(all_token, gain_ref, hidden, squares):
@@ -347,7 +316,7 @@
         out_shape=(
             jax.ShapeDtypeStruct((ZL * YN,) + weight_block.shape, jnp.bfloat16),
             jax.ShapeDtypeStruct((TOK, 256), jnp.bfloat16),
-            jax.ShapeDtypeStruct((HALF, 128), jnp.bfloat16),
+            jax.ShapeDtypeStruct((TOK, 128), jnp.bfloat16),
         ),
         in_specs=[vmem()] * 3,
         out_specs=(vmem(),) * 3,
@@ -356,7 +325,7 @@
             pltpu.VMEM((4 * XN, TOK, FEAT), jnp.bfloat16),
             pltpu.VMEM((FOLD, 128), jnp.float32),
             pltpu.VMEM((TOK, 256), jnp.float32),
-            pltpu.VMEM((TOK, HD), jnp.float32),
+            pltpu.VMEM((TOK, 128), jnp.float32),
             pltpu.SemaphoreType.DMA((ROW_COPIES,)),
             pltpu.SemaphoreType.DMA((ROW_COPIES,)),
             pltpu.SemaphoreType.DMA((COL_COPIES,)),
@@ -370,17 +339,10 @@
 
 
 def kv_kernel(block_ref, out_ref, send_sem, recv_sem, local_sem):
-    core = lax.rem(lax.axis_index("col"), 2)
-    rows = RowGather(
-        block_ref,
-        lambda index: out_ref.at[core, index],
-        send_sem,
-        recv_sem,
-        lambda index: out_ref.at[1 - core, index],
-    )
-    greet(rows.partners() + [(rows.sibling, None)])
+    rows = RowGather(block_ref, lambda index: out_ref.at[index], send_sem, recv_sem)
+    greet(rows.partners())
     rows.along_z(0)
-    own = pltpu.make_async_copy(block_ref, out_ref.at[core, rows.row], local_sem.at[0])
+    own = pltpu.make_async_copy(block_ref, out_ref.at[rows.row], local_sem.at[0])
     own.start()
     for distance in range(1, ZL):
         rows.along_z(distance)
@@ -393,12 +355,12 @@
 def gather_kv(block):
     return pl.pallas_call(
         kv_kernel,
-        out_shape=jax.ShapeDtypeStruct((2, ZL * YN) + block.shape, jnp.bfloat16),
+        out_shape=jax.ShapeDtypeStruct((ZL * YN,) + block.shape, jnp.bfloat16),
         in_specs=[vmem()],
         out_specs=vmem(),
         scratch_shapes=[
-            pltpu.SemaphoreType.DMA((SHARED_COPIES,)),
-            pltpu.SemaphoreType.DMA((SHARED_COPIES,)),
+            pltpu.SemaphoreType.DMA((ROW_COPIES,)),
+            pltpu.SemaphoreType.DMA((ROW_COPIES,)),
             pltpu.SemaphoreType.DMA((1,)),
         ],
         compiler_params=pltpu.CompilerParams(
@@ -524,7 +486,6 @@
     heads = query_weight.shape[1] // HD
     col_index = lax.axis_index("col")
     row_index = lax.axis_index("row")
-    core = col_index % 2
     kv_head = col_index * heads // (HQ // KV)
     half_rows = (spans // 2) * span_rows
     gap = HALF - half_rows - decode_rows
@@ -548,9 +509,13 @@
         )
 
     kv_mine = padded(
-        lax.dynamic_slice(
-            kv_weight, (0, core, kv_head * HD), (kv_weight.shape[0], 1, HD)
-        ).reshape(-1, HD),
+        jnp.concatenate(
+            [
+                lax.dynamic_slice_in_dim(kv_weight[:, which], kv_head * HD, HD, 1)
+                for which in range(2)
+            ],
+            axis=1,
+        ),
         0,
     )
     query_mine = padded(query_weight, 0)
@@ -561,7 +526,7 @@
             query_mine[:, 128:],
             out_mine[:, :128],
             out_mine[:, 128:],
-            jnp.concatenate([kv_mine[: PIECE // 2], kv_mine[PIECE // 2 :]], axis=1),
+            kv_mine,
         ],
         axis=0,
     )
@@ -575,26 +540,19 @@
     gain = (
         padded(norm_gain.astype(jnp.float32).reshape(-1, part), 1).reshape(4 * XN, 1, FEAT)
     )
-    all_weight, queries, kv_block = gather_first(weight_block, token_block, gain)
-    kv_all = gather_kv(kv_block)
+    all_weight, queries, kv_rows = gather_first(weight_block, token_block, gain)
+    kv_all = (
+        gather_kv(jnp.concatenate([kv_rows[:half_rows], kv_rows[HALF : HALF + half_rows]], axis=0))
+        .reshape(-1, spans, span_rows, 2 * HD)
+        .transpose(1, 0, 2, 3)
+        .reshape(spans, -1, 2 * HD)
+    )
     score_scale = 1.0 / math.sqrt(HD)
     sink = sink_logits.astype(jnp.float32)
     query_pre = jnp.concatenate(
         [queries[:half_rows], queries[HALF : HALF + half_rows]], axis=0
     ).reshape(spans, span_rows, heads, HD)
-    key_pair, value_pair = [
-        jnp.concatenate(
-            [
-                kv_all[which, :, :half_rows, side * HD : (side + 1) * HD]
-                .reshape(-1, spans // 2, span_rows, HD)
-                .transpose(1, 0, 2, 3)
-                .reshape(spans // 2, -1, HD)
-                for side in range(2)
-            ],
-            axis=0,
-        )
-        for which in range(2)
-    ]
+    key_pair, value_pair = kv_all[..., :HD], kv_all[..., HD:]
     positions = row_index * span_rows + jnp.arange(span_rows, dtype=jnp.int32)
     scores = (
         jnp.einsum("sqgd,spd->sgqp", query_pre, key_pair, preferred_element_type=jnp.float32)
@@ -619,9 +577,8 @@
         .astype(jnp.bfloat16)
     )
     query_dec = queries[half_rows : half_rows + decode_rows].reshape(decode_rows, heads, HD)
-    new_rows = lax.dynamic_index_in_dim(kv_all, row_index, 1, keepdims=False)
-    key_new = new_rows[0, half_rows : half_rows + decode_rows, :HD]
-    value_new = new_rows[1, half_rows : half_rows + decode_rows, :HD]
+    new_rows = kv_rows[half_rows : half_rows + decode_rows]
+    key_new, value_new = new_rows[:, :HD], new_rows[:, HD:]
     table = page_table.reshape(decode_rows, -1)
     page_len = key_pool.shape[1]
     key_mine = lax.dynamic_slice_in_dim(key_pool, kv_head * HD, HD, 2)

time: 177 us -> 164 us (0.927)
  local copies, waits for them, and re-layouts: 31.8 us -> 16.3 us
  Pallas kernels: 131 us -> 133 us
    transpose x4 -> x0, local copies, waits for them, and re-layouts: 9.53 us -> none  [body(): key_pair, value_pair = [jnp.concatenate([kv_all[which, :, :half_rows, sid...]
    reshape x4 -> x1, local copies, waits for them, and re-layouts: 4.88 us -> 0.17 us  [body(): kv_all = gather_kv(jnp.concatenate([kv_rows[:half_rows], kv_rows[HALF:HAL...]
    pallas_call x1, Pallas kernels: 69.1 us -> 71.8 us  [gather_first(): pl.pallas_call(gather_kernel, out_shape=(jax.ShapeDtypeStruct((ZL * YN,)...]
    unnamed x17 -> x9, local copies, waits for them, and re-layouts: 7.28 us -> 7.47 us
where the time goes in v3:
time: 164 us; the launch traced here: 163 us
  Pallas kernels  133 us (81%)
  local copies, waits for them, and re-layouts  16.3 us (10%)
  other arithmetic  7.18 us (4%)
  matrix products  5.28 us (3%)
    pallas_call x1, Pallas kernels, gather_first(): pl.pallas_call(gather_kernel, out_shape=(jax.ShapeDtypeStruct((ZL * YN,)...  71.8 us
    pallas_call x1, Pallas kernels, gather_kv(): pl.pallas_call(kv_kernel, out_shape=jax.ShapeDtypeStruct((ZL * YN,) + blo...  34.4 us
    pallas_call x1, Pallas kernels, project_out(): pl.pallas_call(out_kernel, out_shape=jax.ShapeDtypeStruct(block, jnp.bflo...  27.4 us
    unnamed x9, local copies, waits for them, and re-layouts  7.47 us

profile of v3, /device:TPU:2, one launch (start us, length us, event | category | flops | bytes accessed | tf_op | source)
XLA Modules:
  0.0 163.2 jit_solution(2681579056853977800)
XLA Ops:
  0.7 1.3 fusion.43
  2.0 0.2 constant_dynamic-slice_fusion.2
  2.2 0.7 fusion.26
  2.9 0.8 fusion.27
  3.7 0.8 fusion.28
  4.4 0.8 fusion.29
  5.2 0.1 fusion.31.weight_ref
  5.3 0.9 fusion.46
  6.2 0.7 concatenate.41
  6.9 0.1 slice.157
  7.0 0.1 pad_slice_fusion.5
  7.1 0.7 slice_select_fusion
  7.8 0.1 fusion.23.token_ref
  7.9 0.8 reshape.116
  8.7 0.1 reshape.128.gain_ref
  8.8 71.8 %shard_map.122 = (bf16[32,480,128]{2,1,0:T(8,128)(2,1)S(1)}, bf16[272,256]{1,0:T(8,128)(2,1)S(1)}, bf16[272,128]{1,0:T(8,128)(2,1)S(1)}) custom-call(bf16[480,128]{1,0:T(8,128)(2,1)S(1)} %fusion.31.weight_ref, bf16[408,128]{1,0:T(8,128)(2,1)S(1)} %fusion.23.token_ref, f32[16,1,192]{2,1,0:T(1,128)S(1)} %reshape.128.gain_ref), custom_call_target="tpu_custom_call" | custom-call | tf_op jit(solution)/shard_map/pallas_call | solution.py:314
  80.6 1.9 %copy-done = bf16[32,480,128]{2,1,0:T(8,128)(2,1)} copy-done((bf16[32,480,128]{2,1,0:T(8,128)(2,1)}, bf16[32,480,128]{2,1,0:T(8,128)(2,1)S(1)}, u32[]{:S(2)}) %copy-start) | copy-done | bytes 3932184
  82.5 0.1 reshape.122
  82.6 0.1 fusion.36
  82.7 1.4 constant_dynamic-slice_fusion
  84.2 0.5 broadcast.106
  84.7 1.3 reduce.3
  86.0 0.1 reshape.123
  86.1 0.1 reshape.131
  86.2 0.6 gather_fusion
  86.8 0.7 iota_compare_fusion.3
  87.5 0.3 fusion.49
  87.9 0.7 convert_element_type.39
  88.6 0.2 fusion.32
  88.7 0.6 gather_fusion.1
  89.4 0.2 fusion.12
  89.6 0.1 convert_element_type.47
  89.7 0.2 reshape.121
  89.9 34.4 %shard_map.123 = bf16[32,256,128]{2,1,0:T(8,128)(2,1)S(1)} custom-call(bf16[256,128]{1,0:T(8,128)(2,1)S(1)} %pad_maximum_fusion.4.block_ref), custom_call_target="tpu_custom_call" | custom-call | tf_op jit(solution)/shard_map/pallas_call | solution.py:356
  124.3 0.2 copy.23
  124.5 0.1 iota_compare_fusion
  124.6 1.5 fusion.2
  126.2 2.2 %fusion = f32[4,4,64]{2,1,0:T(4,128)S(1)} fusion(f32[4,2048,64,4]{1,2,3,0:T(8,128)S(1)} %get-tuple-element.29, f32[4,4,64]{2,1,0:T(4,128)S(1)} %broadcast_maximum_fusion, pred[64,2048]{1,0:T(8,128)(4,1)S(1)} %iota_compare_fusion), kind=kLoop, calls=%fused_computation.4 | loop fusion | flops 8387584 | bytes 8527872 | tf_op jit(solution)/shard_map/reduce_sum | solution.py:566
  128.5 3.1 %fusion.16 = bf16[4,64,4,64]{3,1,2,0:T(8,128)(2,1)S(1)} fusion(bf16[4,2048,128]{2,1,0:T(8,128)(2,1)S(1)} %bitcast.74, f32[4,2048,64,4]{1,2,3,0:T(8,128)S(1)} %get-tuple-element.29, f32[4,4,64]{2,1,0:T(4,128)S(1)} %broadcast_maximum_fusion, pred[64,2048]{1,0:T(8,128)(4,1)S(1)} %iota_compare_fusion, f32[4,64,4]{1,2,0:T(4,128)S(1)} %add_bitcast_fusion), kind=kOutput, calls=%fused_computation.19 | convolution fusion | flops 276955136 | bytes 10756096 | tf_op jit(solution)/shard_map/sgqp,spd->sgqd/dot_general | solution.py:567
  131.6 0.1 copy.27
  131.7 0.1 slice.138
  131.9 0.1 copy.30
  132.0 0.1 slice.143
  132.2 2.1 %copy-done.1 = bf16[32,480,128]{2,1,0:T(8,128)(2,1)S(1)} copy-done((bf16[32,480,128]{2,1,0:T(8,128)(2,1)S(1)}, bf16[32,480,128]{2,1,0:T(8,128)(2,1)}, u32[]{:S(2)}) %copy-start.1) | copy-done | bytes 3932184
  134.3 27.4 %shard_map.124 = bf16[408,128]{1,0:T(8,128)(2,1)S(1)} custom-call(bf16[272,256]{1,0:T(8,128)(2,1)S(1)} %concatenate.47.att_ref, bf16[32,480,128]{2,1,0:T(8,128)(2,1)S(1)} %copy-done.1, bf16[408,128]{1,0:T(8,128)(2,1)S(1)} %fusion.23.token_ref), custom_call_target="tpu_custom_call" | custom-call | tf_op jit(solution)/shard_map/pallas_call | solution.py:449
  161.8 0.1 fusion.22
  161.9 0.7 pad_maximum_fusion.2
  162.6 0.6 slice.164
  (29 shorter events, 0.5 us)
Async XLA Ops:
  80.6 1.9 %copy-start = (bf16[32,480,128]{2,1,0:T(8,128)(2,1)}, bf16[32,480,128]{2,1,0:T(8,128)(2,1)S(1)}, u32[]{:S(2)}) copy-start(bf16[32,480,128]{2,1,0:T(8,128)(2,1)S(1)} %get-tuple-element.7.weight_ref) | copy-start | bytes 11796484
  132.2 2.1 %copy-start.1 = (bf16[32,480,128]{2,1,0:T(8,128)(2,1)S(1)}, bf16[32,480,128]{2,1,0:T(8,128)(2,1)}, u32[]{:S(2)}) copy-start(bf16[32,480,128]{2,1,0:T(8,128)(2,1)} %copy-done) | copy-start | bytes 11796484

commit v4 on v3

--- a/solution.py
+++ b/solution.py
@@ -155,6 +155,36 @@
         self.net.finish()
 
 
+class Halves:
+    def __init__(self, block, out, sems):
+        part = block.shape[0] // 2
+        self.halves = [
+            RowGather(
+                block.at[pl.ds(which * part, part)],
+                lambda index, first=which * part: out.at[index, pl.ds(first, part)],
+                sems[2 * which],
+                sems[2 * which + 1],
+            )
+            for which in range(2)
+        ]
+        self.row = self.halves[0].row
+
+    def partners(self):
+        return self.halves[0].partners()
+
+    def along_z(self, distance):
+        for half in self.halves:
+            half.along_z(distance)
+
+    def along_y(self, distance):
+        for half in self.halves:
+            half.along_y(distance)
+
+    def last(self):
+        for half in self.halves:
+            half.last()
+
+
 class ColGather:
     def __init__(self, block, out, send_sem, recv_sem):
         row, col = lax.axis_index("row"), lax.axis_index("col")
@@ -265,9 +295,9 @@
 
 def gather_kernel(
     weight_ref, token_ref, gain_ref, all_weight, query_ref, kv_ref, all_token, hidden, squares,
-    query_sum, kv_sum, rs, rr, cs, cr, local_sem,
+    query_sum, kv_sum, rs, rr, rs2, rr2, cs, cr, local_sem,
 ):
-    rows = RowGather(weight_ref, lambda index: all_weight.at[index], rs, rr)
+    rows = Halves(weight_ref, all_weight, (rs, rr, rs2, rr2))
     cols = ColGather(token_ref, all_token, cs, cr)
     greet(rows.partners() + cols.partners())
     cols.own(0)
@@ -328,6 +358,8 @@
             pltpu.VMEM((TOK, 128), jnp.float32),
             pltpu.SemaphoreType.DMA((ROW_COPIES,)),
             pltpu.SemaphoreType.DMA((ROW_COPIES,)),
+            pltpu.SemaphoreType.DMA((ROW_COPIES,)),
+            pltpu.SemaphoreType.DMA((ROW_COPIES,)),
             pltpu.SemaphoreType.DMA((COL_COPIES,)),
             pltpu.SemaphoreType.DMA((COL_COPIES,)),
             pltpu.SemaphoreType.DMA((2,)),
@@ -338,8 +370,8 @@
     )(weight_block, token_block, gain)
 
 
-def kv_kernel(block_ref, out_ref, send_sem, recv_sem, local_sem):
-    rows = RowGather(block_ref, lambda index: out_ref.at[index], send_sem, recv_sem)
+def kv_kernel(block_ref, out_ref, rs, rr, rs2, rr2, local_sem):
+    rows = Halves(block_ref, out_ref, (rs, rr, rs2, rr2))
     greet(rows.partners())
     rows.along_z(0)
     own = pltpu.make_async_copy(block_ref, out_ref.at[rows.row], local_sem.at[0])
@@ -359,6 +391,8 @@
         in_specs=[vmem()],
         out_specs=vmem(),
         scratch_shapes=[
+            pltpu.SemaphoreType.DMA((ROW_COPIES,)),
+            pltpu.SemaphoreType.DMA((ROW_COPIES,)),
             pltpu.SemaphoreType.DMA((ROW_COPIES,)),
             pltpu.SemaphoreType.DMA((ROW_COPIES,)),
             pltpu.SemaphoreType.DMA((1,)),

time: 164 us -> 159 us (0.970)
  the two profiles are of different devices: /device:TPU:2 before, /device:TPU:26 now
where the time goes in v4:
time: 159 us
  Pallas kernels  129 us (81%)
  local copies, waits for them, and re-layouts  16.3 us (10%)
  other arithmetic  7.18 us (5%)
  matrix products  5.27 us (3%)
    pallas_call x1, Pallas kernels, gather_first(): pl.pallas_call(gather_kernel, out_shape=(jax.ShapeDtypeStruct((ZL * YN,)...  67.9 us
    pallas_call x1, Pallas kernels, gather_kv(): pl.pallas_call(kv_kernel, out_shape=jax.ShapeDtypeStruct((ZL * YN,) + blo...  34 us
    pallas_call x1, Pallas kernels, project_out(): pl.pallas_call(out_kernel, out_shape=jax.ShapeDtypeStruct(block, jnp.bflo...  27.2 us
    unnamed x9, local copies, waits for them, and re-layouts  7.47 us

profile of v4, /device:TPU:26, one launch (start us, length us, event | category | flops | bytes accessed | tf_op | source)
XLA Modules:
  0.0 158.8 jit_solution(11306256773722175098)
XLA Ops:
  0.7 1.3 fusion.43
  2.0 0.2 constant_dynamic-slice_fusion.2
  2.2 0.7 fusion.26
  2.9 0.8 fusion.27
  3.7 0.8 fusion.28
  4.4 0.8 fusion.29
  5.2 0.1 fusion.31.weight_ref
  5.3 0.9 fusion.46
  6.2 0.7 concatenate.41
  6.9 0.1 slice.157
  7.0 0.1 pad_slice_fusion.5
  7.1 0.7 slice_select_fusion
  7.8 0.1 fusion.23.token_ref
  7.9 0.8 reshape.116
  8.7 0.1 reshape.128.gain_ref
  8.8 67.9 %shard_map.122 = (bf16[32,480,128]{2,1,0:T(8,128)(2,1)S(1)}, bf16[272,256]{1,0:T(8,128)(2,1)S(1)}, bf16[272,128]{1,0:T(8,128)(2,1)S(1)}) custom-call(bf16[480,128]{1,0:T(8,128)(2,1)S(1)} %fusion.31.weight_ref, bf16[408,128]{1,0:T(8,128)(2,1)S(1)} %fusion.23.token_ref, f32[16,1,192]{2,1,0:T(1,128)S(1)} %reshape.128.gain_ref), custom_call_target="tpu_custom_call" | custom-call | tf_op jit(solution)/shard_map/pallas_call | solution.py:344
  76.8 1.9 %copy-done = bf16[32,480,128]{2,1,0:T(8,128)(2,1)} copy-done((bf16[32,480,128]{2,1,0:T(8,128)(2,1)}, bf16[32,480,128]{2,1,0:T(8,128)(2,1)S(1)}, u32[]{:S(2)}) %copy-start) | copy-done | bytes 3932184
  78.6 0.1 reshape.122
  78.8 0.1 fusion.36
  78.9 1.4 constant_dynamic-slice_fusion
  80.3 0.5 broadcast.106
  80.8 1.3 reduce.3
  82.1 0.1 reshape.123
  82.2 0.1 reshape.131
  82.3 0.6 gather_fusion
  83.0 0.7 iota_compare_fusion.3
  83.7 0.3 fusion.49
  84.0 0.7 convert_element_type.39
  84.7 0.2 fusion.32
  84.9 0.6 gather_fusion.1
  85.5 0.2 fusion.12
  85.8 0.1 convert_element_type.47
  85.9 0.2 reshape.121
  86.1 34.0 %shard_map.123 = bf16[32,256,128]{2,1,0:T(8,128)(2,1)S(1)} custom-call(bf16[256,128]{1,0:T(8,128)(2,1)S(1)} %pad_maximum_fusion.4.block_ref), custom_call_target="tpu_custom_call" | custom-call | tf_op jit(solution)/shard_map/pallas_call | solution.py:388
  120.1 0.2 copy.23
  120.3 0.1 iota_compare_fusion
  120.4 1.5 fusion.2
  122.0 2.2 %fusion = f32[4,4,64]{2,1,0:T(4,128)S(1)} fusion(f32[4,2048,64,4]{1,2,3,0:T(8,128)S(1)} %get-tuple-element.29, f32[4,4,64]{2,1,0:T(4,128)S(1)} %broadcast_maximum_fusion, pred[64,2048]{1,0:T(8,128)(4,1)S(1)} %iota_compare_fusion), kind=kLoop, calls=%fused_computation.4 | loop fusion | flops 8387584 | bytes 8527872 | tf_op jit(solution)/shard_map/reduce_sum | solution.py:600
  124.3 3.1 %fusion.16 = bf16[4,64,4,64]{3,1,2,0:T(8,128)(2,1)S(1)} fusion(bf16[4,2048,128]{2,1,0:T(8,128)(2,1)S(1)} %bitcast.74, f32[4,2048,64,4]{1,2,3,0:T(8,128)S(1)} %get-tuple-element.29, f32[4,4,64]{2,1,0:T(4,128)S(1)} %broadcast_maximum_fusion, pred[64,2048]{1,0:T(8,128)(4,1)S(1)} %iota_compare_fusion, f32[4,64,4]{1,2,0:T(4,128)S(1)} %add_bitcast_fusion), kind=kOutput, calls=%fused_computation.19 | convolution fusion | flops 276955136 | bytes 10756096 | tf_op jit(solution)/shard_map/sgqp,spd->sgqd/dot_general | solution.py:601
  127.4 0.1 copy.27
  127.5 0.1 slice.138
  127.7 0.1 copy.30
  127.8 0.1 slice.143
  128.0 2.1 %copy-done.1 = bf16[32,480,128]{2,1,0:T(8,128)(2,1)S(1)} copy-done((bf16[32,480,128]{2,1,0:T(8,128)(2,1)S(1)}, bf16[32,480,128]{2,1,0:T(8,128)(2,1)}, u32[]{:S(2)}) %copy-start.1) | copy-done | bytes 3932184
  130.1 27.2 %shard_map.124 = bf16[408,128]{1,0:T(8,128)(2,1)S(1)} custom-call(bf16[272,256]{1,0:T(8,128)(2,1)S(1)} %concatenate.47.att_ref, bf16[32,480,128]{2,1,0:T(8,128)(2,1)S(1)} %copy-done.1, bf16[408,128]{1,0:T(8,128)(2,1)S(1)} %fusion.23.token_ref), custom_call_target="tpu_custom_call" | custom-call | tf_op jit(solution)/shard_map/pallas_call | solution.py:483
  157.4 0.1 fusion.22
  157.5 0.7 pad_maximum_fusion.2
  158.2 0.6 slice.164
  (29 shorter events, 0.5 us)
Async XLA Ops:
  76.7 1.9 %copy-start = (bf16[32,480,128]{2,1,0:T(8,128)(2,1)}, bf16[32,480,128]{2,1,0:T(8,128)(2,1)S(1)}, u32[]{:S(2)}) copy-start(bf16[32,480,128]{2,1,0:T(8,128)(2,1)S(1)} %get-tuple-element.7.weight_ref) | copy-start | bytes 11796484
  128.0 2.1 %copy-start.1 = (bf16[32,480,128]{2,1,0:T(8,128)(2,1)S(1)}, bf16[32,480,128]{2,1,0:T(8,128)(2,1)}, u32[]{:S(2)}) copy-start(bf16[32,480,128]{2,1,0:T(8,128)(2,1)} %copy-done) | copy-start | bytes 11796484
